TPU v7x, 512 devices: a whole 4x4x16 slice. The times are simulated.
512 devices in a mesh: blk: 64 (over x, z), grp: 8 (over y, core).
Axes of the slice: x: 4, y: 4, z: 16, core: 2. Of those that a mesh axis runs over, the one named last changes fastest.
Arguments:
- points: bfloat16 [8, 65536, 128], P('grp', 'blk'), may hold values from -4 to 4
- start_panel: bfloat16 [8, 64, 65536], P('grp', None, 'blk'), may hold values from -6 to 6
- seventh: int32 [8, 65536], P('grp', 'blk'), may hold values from 0 to 255, as said below
- neighbours: int32 [8, 256, 16], P('grp'), may hold values from 0 to 255, as said below
- counts: int32 [8, 256], P('grp'), may hold values from 1 to 16, as said below
Outputs:
- ortho_basis: float32 [8, 64, 65536], P('grp', None, 'blk')
- r_factor: float32 [64, 64], replicated
Inputs may be any that keep to these rules, and one draw needn't show every extreme that they name: `seventh`: A point's position within its own block, never the point's own position. `neighbours`: block numbers within the group; block B's owner is B // 4. The listed entries of a block are distinct, never the block itself, and each is owned by an owner whose number differs from B's owner by at most 4 modulo 64. The entries after the listed ones are block numbers of the group and are not used. Of the blocks of one owner, at most 2 are listed by the blocks of another owner together, and exactly 2 for some pairs of owners. `counts`: some block of every group lists 16 blocks.
All inputs are finite; a program needn't handle non-finite values.
Results may differ from a plain program's by a relative error of at most 0.0082.
Values may be sent and summed in bfloat16 or wider, within the bound.
A program may use at most 64 MiB of HBM per device.

v0:
```python
import math

import jax
import jax.numpy as jnp
from jax import lax
from jax.sharding import PartitionSpec as P

E = 128
K = 64
BS = 256
SLOTS = 16
REACH = 4


def passed_along(block, axis, distance):
    devices = range(lax.axis_size(axis))
    route = [((i - distance) % len(devices), i) for i in devices]
    return lax.ppermute(block, axis, route)


def fetch_whole(send_points, send_panel, send_scales, offset):
    return passed_along((send_points, send_panel, send_scales), "blk", offset)


def tile_terms(
    row_points, row_scales, row_norms, col_points, col_panel, col_scales, col_norms, pair_mask
):
    inner_prod = jnp.einsum(
        "pe,cqe->cpq", row_points, col_points, preferred_element_type=jnp.float32
    )
    distance = row_norms[None, :, None] + col_norms[:, None, :] - 2.0 * inner_prod
    denom_scale = (
        row_scales.astype(jnp.float32)[None, :, None] * col_scales.astype(jnp.float32)[:, None, :]
    )
    affinity = jnp.exp(-distance / denom_scale) * pair_mask[:, None, None]
    weights = affinity.astype(jnp.bfloat16)
    carried = jnp.einsum("cpq,kcq->kp", weights, col_panel, preferred_element_type=jnp.float32)
    return (carried, jnp.sum(affinity, axis=(0, 2)))


def local(points, start_panel, seventh, neighbours, counts):
    cycle_size = lax.axis_size("blk")
    my_index = lax.axis_index("blk")
    per_dev = points.shape[1] // BS
    own_points = points[0].reshape(per_dev, BS, E)
    partner_pos = seventh[0].reshape(per_dev, BS)
    partner = jnp.take_along_axis(own_points, partner_pos[:, :, None], axis=1)
    difference = own_points.astype(jnp.float32) - partner.astype(jnp.float32)
    scales = jnp.sqrt(jnp.sum(difference * difference, axis=-1) + 1e-06).astype(jnp.bfloat16)
    as_float = own_points.astype(jnp.float32)
    sq_norm = jnp.sum(as_float * as_float, axis=-1)
    own_panel = start_panel[0].reshape(K, per_dev, BS)
    block_lists = neighbours[0]
    live_mask = jnp.arange(SLOTS, dtype=jnp.int32)[None, :] < counts[0][:, None]
    my_lists = lax.dynamic_slice_in_dim(block_lists, my_index * per_dev, per_dev, 0)
    my_live = lax.dynamic_slice_in_dim(live_mask, my_index * per_dev, per_dev, 0)

    def accumulate(totals, col_points, col_panel, col_scales, col_ids):
        pair_mask = jnp.any(
            (my_lists[:, :, None] == col_ids[None, None, :]) & my_live[:, :, None], axis=1
        ).astype(jnp.float32)
        col_float = col_points.astype(jnp.float32)
        col_norms = jnp.sum(col_float * col_float, axis=-1)

        def per_block(inputs):
            row_points, row_scales, row_norms, row_mask = inputs
            return tile_terms(
                row_points,
                row_scales,
                row_norms,
                col_points,
                col_panel,
                col_scales,
                col_norms,
                row_mask,
            )

        carried, degree = lax.map(per_block, (own_points, scales, sq_norm, pair_mask))
        return (totals[0] + carried, totals[1] + degree)

    totals = (jnp.zeros((per_dev, K, BS), jnp.float32), jnp.zeros((per_dev, BS), jnp.float32))
    local_ids = my_index * per_dev + jnp.arange(per_dev, dtype=jnp.int32)
    totals = accumulate(totals, own_points, own_panel, scales, local_ids)
    for offset in list(range(1, REACH + 1)) + list(range(-REACH, 0)):
        source = (my_index - offset) % cycle_size
        col_points, col_panel, col_scales = fetch_whole(own_points, own_panel, scales, offset)
        col_ids = source * per_dev + jnp.arange(per_dev, dtype=jnp.int32)
        totals = accumulate(totals, col_points, col_panel, col_scales, col_ids)
    carried = jnp.transpose(totals[0], (1, 0, 2))
    degree = 1.0 + totals[1]
    walked = ((own_panel.astype(jnp.float32) + carried) / degree[None, :, :]).reshape(
        K, per_dev * BS
    )
    gram_local = jnp.dot(
        walked, walked.T, precision=lax.Precision.HIGHEST, preferred_element_type=jnp.float32
    )
    gram_matrix = lax.psum(gram_local, ("blk", "grp"))
    lower_factor = jnp.linalg.cholesky(gram_matrix)
    solved = lax.linalg.triangular_solve(lower_factor, walked, left_side=True, lower=True)
    point_total = points.shape[1] * lax.axis_size("blk") * lax.axis_size("grp")
    root_count = math.sqrt(point_total)
    ortho_basis = (solved * root_count)[None]
    r_factor = lower_factor.T / root_count
    return (ortho_basis, r_factor)


def solution(mesh):
    in_specs = (
        P("grp", "blk", None),
        P("grp", None, "blk"),
        P("grp", "blk"),
        P("grp", None, None),
        P("grp", None),
    )
    out_specs = (P("grp", None, "blk"), P())
    return jax.shard_map(local, mesh=mesh, in_specs=in_specs, out_specs=out_specs, check_vma=False)
```

profile of v0, /device:TPU:1, one launch (start us, length us, event | category | flops | bytes accessed | tf_op | source)
XLA Modules:
  0.0 331.3 jit_solution(13664249299728064872)
XLA Ops:
  6.0 4.9 %collective-permute-start.5 = (bf16[64,4,256]{2,1,0:T(4,128)(2,1)S(1)}, bf16[64,4,256]{2,1,0:T(4,128)(2,1)S(1)}, u32[]{:S(2)}, u32[]{:S(2)}) collective-permute-start(bf16[64,4,256]{2,1,0:T(4,128)(2,1)S(1)} %reshape_squeeze.6), channel_id=1, source_target_pairs={{496,0},{504,8},{0,16},{8,24},{16,32},{24,40},{32,48},{40,56},{48,... | collective-permute-start | bytes 393224 | tf_op jit(solution)/shard_map/ppermute | solution.py:18
  10.9 7.5 %collective-permute-start.8 = (bf16[64,4,256]{2,1,0:T(4,128)(2,1)S(1)}, bf16[64,4,256]{2,1,0:T(4,128)(2,1)S(1)}, u32[]{:S(2)}, u32[]{:S(2)}) collective-permute-start(bf16[64,4,256]{2,1,0:T(4,128)(2,1)S(1)} %reshape_squeeze.6), channel_id=1, source_target_pairs={{488,0},{496,8},{504,16},{0,24},{8,32},{16,40},{24,48},{32,56},{40... | collective-permute-start | bytes 393224 | tf_op jit(solution)/shard_map/ppermute | solution.py:18
  18.4 7.0 %collective-permute-start.11 = (bf16[64,4,256]{2,1,0:T(4,128)(2,1)S(1)}, bf16[64,4,256]{2,1,0:T(4,128)(2,1)S(1)}, u32[]{:S(2)}, u32[]{:S(2)}) collective-permute-start(bf16[64,4,256]{2,1,0:T(4,128)(2,1)S(1)} %reshape_squeeze.6), channel_id=1, source_target_pairs={{480,0},{488,8},{496,16},{504,24},{0,32},{8,40},{16,48},{24,56},{3... | collective-permute-start | bytes 393224 | tf_op jit(solution)/shard_map/ppermute | solution.py:18
  30.2 6.8 %gather_fusion = bf16[1024,128]{1,0:T(8,128)(2,1)S(1)} fusion(bf16[4,256,128]{2,1,0:T(8,128)(2,1)} %bitcast.90, s32[1024]{0:T(1024)S(1)} %bitcast.504), kind=kCustom, calls=%fused_computation | custom fusion | bytes 532480 | tf_op jit(solution)/shard_map/jit(take_along_axis)/gather | solution.py:47
  40.1 5.2 %collective-permute-start.14 = (bf16[64,4,256]{2,1,0:T(4,128)(2,1)S(1)}, bf16[64,4,256]{2,1,0:T(4,128)(2,1)S(1)}, u32[]{:S(2)}, u32[]{:S(2)}) collective-permute-start(bf16[64,4,256]{2,1,0:T(4,128)(2,1)S(1)} %reshape_squeeze.6), channel_id=1, source_target_pairs={{32,0},{40,8},{48,16},{56,24},{64,32},{72,40},{80,48},{88,56},{96,... | collective-permute-start | bytes 393224 | tf_op jit(solution)/shard_map/ppermute | solution.py:18
  55.7 13.1 %while.109 = (s32[]{:T(128)}, f32[4,64,256]{2,1,0:T(8,128)S(1)}, f32[4,256]{1,0:T(4,128)S(1)}, f32[4,256]{1,0:T(4,128)S(1)}, bf16[4,256,128]{2,1,0:T(8,128)(2,1)...) while((s32[]{:T(128)}, f32[4,64,256]{2,1,0:T(8,128)S(1)}, ...), condition=%wide.region_5.6_spmd, body=%wide.region_3.0_spmd.sunk | while | flops 103023616 | bytes 1596585 | solution.py:78
  73.7 5.2 %collective-permute-start.3 = (bf16[4,256,128]{2,1,0:T(8,128)(2,1)}, bf16[4,256,128]{2,1,0:T(8,128)(2,1)S(1)}, u32[]{:S(2)}, u32[]{:S(2)}) collective-permute-start(bf16[4,256,128]{2,1,0:T(8,128)(2,1)} %bitcast.90), channel_id=1, source_target_pairs={{496,0},{504,8},{0,16},{8,24},{16,32},{24,40},{32,48},{40,56},{48,... | collective-permute-start | bytes 786440 | tf_op jit(solution)/shard_map/ppermute | solution.py:18
  79.0 5.9 %collective-permute-start.7 = (bf16[4,256]{1,0:T(4,128)(2,1)}, bf16[4,256]{1,0:T(4,128)(2,1)S(1)}, u32[]{:S(2)}, u32[]{:S(2)}) collective-permute-start(bf16[4,256]{1,0:T(4,128)(2,1)} %convert_element_type.264), channel_id=1, source_target_pairs={{488,0},{496,8},{504,16},{0,24},{8,32},{16,40},{24,48},{32,56},{40... | collective-permute-start | bytes 6152 | tf_op jit(solution)/shard_map/ppermute | solution.py:18
  89.5 9.6 %while.110 = (s32[]{:T(128)}, f32[4,64,256]{2,1,0:T(8,128)S(1)}, f32[4,256]{1,0:T(4,128)S(1)}, f32[4,256]{1,0:T(4,128)S(1)}, f32[4,256]{1,0:T(4,128)S(1)}, /*ind...) while((s32[]{:T(128)}, f32[4,64,256]{2,1,0:T(8,128)S(1)}, ...), condition=%wide.region_10.11_spmd, body=%wide.region_8.10_spmd.sunk | while | flops 103023616 | bytes 1596609 | solution.py:78
  99.2 4.9 %collective-permute-start.9 = (bf16[4,256,128]{2,1,0:T(8,128)(2,1)}, bf16[4,256,128]{2,1,0:T(8,128)(2,1)S(1)}, u32[]{:S(2)}, u32[]{:S(2)}) collective-permute-start(bf16[4,256,128]{2,1,0:T(8,128)(2,1)} %bitcast.90), channel_id=1, source_target_pairs={{480,0},{488,8},{496,16},{504,24},{0,32},{8,40},{16,48},{24,56},{3... | collective-permute-start | bytes 786440 | tf_op jit(solution)/shard_map/ppermute | solution.py:18
  104.3 6.4 %collective-permute-start.13 = (bf16[4,256]{1,0:T(4,128)(2,1)}, bf16[4,256]{1,0:T(4,128)(2,1)S(1)}, u32[]{:S(2)}, u32[]{:S(2)}) collective-permute-start(bf16[4,256]{1,0:T(4,128)(2,1)} %convert_element_type.264), channel_id=1, source_target_pairs={{32,0},{40,8},{48,16},{56,24},{64,32},{72,40},{80,48},{88,56},{96,... | collective-permute-start | bytes 6152 | tf_op jit(solution)/shard_map/ppermute | solution.py:18
  110.8 9.6 %while.111 = (s32[]{:T(128)}, f32[4,64,256]{2,1,0:T(8,128)S(1)}, f32[4,256]{1,0:T(4,128)S(1)}, f32[4,256]{1,0:T(4,128)S(1)}, f32[4,256]{1,0:T(4,128)S(1)}, /*ind...) while((s32[]{:T(128)}, f32[4,64,256]{2,1,0:T(8,128)S(1)}, ...), condition=%wide.region_15.16_spmd, body=%wide.region_13.15_spmd.sunk | while | flops 103023616 | bytes 1596609 | solution.py:78
  120.4 7.3 %collective-permute-start.12 = (bf16[4,256,128]{2,1,0:T(8,128)(2,1)}, bf16[4,256,128]{2,1,0:T(8,128)(2,1)S(1)}, u32[]{:S(2)}, u32[]{:S(2)}) collective-permute-start(bf16[4,256,128]{2,1,0:T(8,128)(2,1)} %bitcast.90), channel_id=1, source_target_pairs={{32,0},{40,8},{48,16},{56,24},{64,32},{72,40},{80,48},{88,56},{96,... | collective-permute-start | bytes 786440 | tf_op jit(solution)/shard_map/ppermute | solution.py:18
  127.9 5.9 %collective-permute-start.16 = (bf16[4,256]{1,0:T(4,128)(2,1)}, bf16[4,256]{1,0:T(4,128)(2,1)S(1)}, u32[]{:S(2)}, u32[]{:S(2)}) collective-permute-start(bf16[4,256]{1,0:T(4,128)(2,1)} %convert_element_type.264), channel_id=1, source_target_pairs={{24,0},{32,8},{40,16},{48,24},{56,32},{64,40},{72,48},{80,56},{88,... | collective-permute-start | bytes 6152 | tf_op jit(solution)/shard_map/ppermute | solution.py:18
  133.9 9.6 %while.112 = (s32[]{:T(128)}, f32[4,64,256]{2,1,0:T(8,128)S(1)}, f32[4,256]{1,0:T(4,128)S(1)}, f32[4,256]{1,0:T(4,128)S(1)}, f32[4,256]{1,0:T(4,128)S(1)}, /*ind...) while((s32[]{:T(128)}, f32[4,64,256]{2,1,0:T(8,128)S(1)}, ...), condition=%wide.region_20.21_spmd, body=%wide.region_18.20_spmd.sunk | while | flops 103023616 | bytes 1596609 | solution.py:78
  148.1 9.6 %while.113 = (s32[]{:T(128)}, f32[4,64,256]{2,1,0:T(8,128)S(1)}, f32[4,256]{1,0:T(4,128)S(1)}, f32[4,256]{1,0:T(4,128)S(1)}, f32[4,256]{1,0:T(4,128)S(1)}, /*ind...) while((s32[]{:T(128)}, f32[4,64,256]{2,1,0:T(8,128)S(1)}, ...), condition=%wide.region_25.26_spmd, body=%wide.region_23.25_spmd.sunk | while | flops 103023616 | bytes 1596609 | solution.py:78
  157.7 4.8 %collective-permute-start.18 = (bf16[4,256,128]{2,1,0:T(8,128)(2,1)}, bf16[4,256,128]{2,1,0:T(8,128)(2,1)S(1)}, u32[]{:S(2)}, u32[]{:S(2)}) collective-permute-start(bf16[4,256,128]{2,1,0:T(8,128)(2,1)} %bitcast.90), channel_id=1, source_target_pairs={{16,0},{24,8},{32,16},{40,24},{48,32},{56,40},{64,48},{72,56},{80,... | collective-permute-start | bytes 786440 | tf_op jit(solution)/shard_map/ppermute | solution.py:18
  165.9 9.6 %while.114 = (s32[]{:T(128)}, f32[4,64,256]{2,1,0:T(8,128)S(1)}, f32[4,256]{1,0:T(4,128)S(1)}, f32[4,256]{1,0:T(4,128)S(1)}, f32[4,256]{1,0:T(4,128)S(1)}, /*ind...) while((s32[]{:T(128)}, f32[4,64,256]{2,1,0:T(8,128)S(1)}, ...), condition=%wide.region_30.31_spmd, body=%wide.region_28.30_spmd.sunk | while | flops 103023616 | bytes 1596609 | solution.py:78
  177.9 9.6 %while.115 = (s32[]{:T(128)}, f32[4,64,256]{2,1,0:T(8,128)S(1)}, f32[4,256]{1,0:T(4,128)S(1)}, f32[4,256]{1,0:T(4,128)S(1)}, f32[4,256]{1,0:T(4,128)S(1)}, /*ind...) while((s32[]{:T(128)}, f32[4,64,256]{2,1,0:T(8,128)S(1)}, ...), condition=%wide.region_35.36_spmd, body=%wide.region_33.35_spmd.sunk | while | flops 103023616 | bytes 1596609 | solution.py:78
  187.8 9.6 %while.116 = (s32[]{:T(128)}, f32[4,64,256]{2,1,0:T(8,128)S(1)}, f32[4,256]{1,0:T(4,128)S(1)}, f32[4,256]{1,0:T(4,128)S(1)}, f32[4,256]{1,0:T(4,128)S(1)}, /*ind...) while((s32[]{:T(128)}, f32[4,64,256]{2,1,0:T(8,128)S(1)}, ...), condition=%wide.region_40.41_spmd, body=%wide.region_38.40_spmd.sunk | while | flops 103023616 | bytes 1596609 | solution.py:78
  198.7 10.2 %while.117 = (s32[]{:T(128)}, f32[4,64,256]{2,1,0:T(8,128)S(1)}, f32[4,256]{1,0:T(4,128)S(1)}, f32[4,256]{1,0:T(4,128)S(1)}, f32[4,256]{1,0:T(4,128)S(1)}, /*ind...) while((s32[]{:T(128)}, f32[4,64,256]{2,1,0:T(8,128)S(1)}, ...), condition=%wide.region_45.46_spmd, body=%wide.region_43.45_spmd.sunk | while | flops 103023616 | bytes 1596609 | solution.py:78
  209.5 107.8 %psum.7 = f32[64,64]{0,1:T(8,128)S(1)} all-reduce(f32[64,64]{0,1:T(8,128)S(1)} %convolution_bitcast_fusion.9), channel_id=1, replica_groups=mesh['blk'=64,'grp'=8] {'blk','grp'}, use_global_device_ids=true, to_apply=%region_46.47 | all-reduce | flops 4096 | bytes 32768 | tf_op jit(solution)/shard_map/psum | solution.py:97
  317.3 5.8 %cholesky.16 = f32[64,64]{1,0:T(8,128)S(1)} custom-call(f32[64,64]{1,0:T(8,128)S(1)} %fusion.123), custom_call_target="Cholesky" | custom-call | tf_op jit(solution)/shard_map/jit(cholesky)/cholesky | solution.py:98
  324.5 4.9 %custom-call.6 = f32[1,64,64]{1,2,0:T(8,128)S(1)} custom-call(f32[1,64,64]{2,1,0:T(8,128)S(1)} %get-tuple-element.1067), custom_call_target="InvertDiagBlocksLowerTriangular" | custom-call | tf_op jit(solution)/shard_map/triangular_solve | solution.py:99
  (371 shorter events, 137.9 us)
Async XLA Ops:
  1.6 38.4 %collective-permute-start.2 = (bf16[64,4,256]{2,1,0:T(4,128)(2,1)S(1)}, bf16[64,4,256]{2,1,0:T(4,128)(2,1)S(1)}, u32[]{:S(2)}, u32[]{:S(2)}) collective-permute-start(bf16[64,4,256]{2,1,0:T(4,128)(2,1)S(1)} %reshape_squeeze.6), channel_id=1, source_target_pairs={{504,0},{0,8},{8,16},{16,24},{24,32},{32,40},{40,48},{48,56},{56,6... | collective-permute-start | bytes 393224 | tf_op jit(solution)/shard_map/ppermute | solution.py:18
  6.0 39.2 %collective-permute-start.5 = (bf16[64,4,256]{2,1,0:T(4,128)(2,1)S(1)}, bf16[64,4,256]{2,1,0:T(4,128)(2,1)S(1)}, u32[]{:S(2)}, u32[]{:S(2)}) collective-permute-start(bf16[64,4,256]{2,1,0:T(4,128)(2,1)S(1)} %reshape_squeeze.6), channel_id=1, source_target_pairs={{496,0},{504,8},{0,16},{8,24},{16,32},{24,40},{32,48},{40,56},{48,... | collective-permute-start | bytes 393224 | tf_op jit(solution)/shard_map/ppermute | solution.py:18
  10.9 37.9 %collective-permute-start.8 = (bf16[64,4,256]{2,1,0:T(4,128)(2,1)S(1)}, bf16[64,4,256]{2,1,0:T(4,128)(2,1)S(1)}, u32[]{:S(2)}, u32[]{:S(2)}) collective-permute-start(bf16[64,4,256]{2,1,0:T(4,128)(2,1)S(1)} %reshape_squeeze.6), channel_id=1, source_target_pairs={{488,0},{496,8},{504,16},{0,24},{8,32},{16,40},{24,48},{32,56},{40... | collective-permute-start | bytes 393224 | tf_op jit(solution)/shard_map/ppermute | solution.py:18
  18.4 34.1 %collective-permute-start.11 = (bf16[64,4,256]{2,1,0:T(4,128)(2,1)S(1)}, bf16[64,4,256]{2,1,0:T(4,128)(2,1)S(1)}, u32[]{:S(2)}, u32[]{:S(2)}) collective-permute-start(bf16[64,4,256]{2,1,0:T(4,128)(2,1)S(1)} %reshape_squeeze.6), channel_id=1, source_target_pairs={{480,0},{488,8},{496,16},{504,24},{0,32},{8,40},{16,48},{24,56},{3... | collective-permute-start | bytes 393224 | tf_op jit(solution)/shard_map/ppermute | solution.py:18
  25.4 59.5 %collective-permute-start = (bf16[4,256,128]{2,1,0:T(8,128)(2,1)}, bf16[4,256,128]{2,1,0:T(8,128)(2,1)S(1)}, u32[]{:S(2)}, u32[]{:S(2)}) collective-permute-start(bf16[4,256,128]{2,1,0:T(8,128)(2,1)} %bitcast.90), channel_id=1, source_target_pairs={{504,0},{0,8},{8,16},{16,24},{24,32},{32,40},{40,48},{48,56},{56,6... | collective-permute-start | bytes 786440 | tf_op jit(solution)/shard_map/ppermute | solution.py:18
  40.1 28.9 %collective-permute-start.14 = (bf16[64,4,256]{2,1,0:T(4,128)(2,1)S(1)}, bf16[64,4,256]{2,1,0:T(4,128)(2,1)S(1)}, u32[]{:S(2)}, u32[]{:S(2)}) collective-permute-start(bf16[64,4,256]{2,1,0:T(4,128)(2,1)S(1)} %reshape_squeeze.6), channel_id=1, source_target_pairs={{32,0},{40,8},{48,16},{56,24},{64,32},{72,40},{80,48},{88,56},{96,... | collective-permute-start | bytes 393224 | tf_op jit(solution)/shard_map/ppermute | solution.py:18
  45.3 25.9 %collective-permute-start.17 = (bf16[64,4,256]{2,1,0:T(4,128)(2,1)S(1)}, bf16[64,4,256]{2,1,0:T(4,128)(2,1)S(1)}, u32[]{:S(2)}, u32[]{:S(2)}) collective-permute-start(bf16[64,4,256]{2,1,0:T(4,128)(2,1)S(1)} %reshape_squeeze.6), channel_id=1, source_target_pairs={{24,0},{32,8},{40,16},{48,24},{56,32},{64,40},{72,48},{80,56},{88,... | collective-permute-start | bytes 393224 | tf_op jit(solution)/shard_map/ppermute | solution.py:18
  48.9 24.9 %collective-permute-start.20 = (bf16[64,4,256]{2,1,0:T(4,128)(2,1)S(1)}, bf16[64,4,256]{2,1,0:T(4,128)(2,1)S(1)}, u32[]{:S(2)}, u32[]{:S(2)}) collective-permute-start(bf16[64,4,256]{2,1,0:T(4,128)(2,1)S(1)} %reshape_squeeze.6), channel_id=1, source_target_pairs={{16,0},{24,8},{32,16},{40,24},{48,32},{56,40},{64,48},{72,56},{80,... | collective-permute-start | bytes 393224 | tf_op jit(solution)/shard_map/ppermute | solution.py:18
  52.5 26.4 %collective-permute-start.23 = (bf16[64,4,256]{2,1,0:T(4,128)(2,1)S(1)}, bf16[64,4,256]{2,1,0:T(4,128)(2,1)S(1)}, u32[]{:S(2)}, u32[]{:S(2)}) collective-permute-start(bf16[64,4,256]{2,1,0:T(4,128)(2,1)S(1)} %reshape_squeeze.6), channel_id=1, source_target_pairs={{8,0},{16,8},{24,16},{32,24},{40,32},{48,40},{56,48},{64,56},{72,6... | collective-permute-start | bytes 393224 | tf_op jit(solution)/shard_map/ppermute | solution.py:18
  68.9 18.6 %collective-permute-start.1 = (bf16[4,256]{1,0:T(4,128)(2,1)}, bf16[4,256]{1,0:T(4,128)(2,1)S(1)}, u32[]{:S(2)}, u32[]{:S(2)}) collective-permute-start(bf16[4,256]{1,0:T(4,128)(2,1)} %convert_element_type.264), channel_id=1, source_target_pairs={{504,0},{0,8},{8,16},{16,24},{24,32},{32,40},{40,48},{48,56},{56,6... | collective-permute-start | bytes 6152 | tf_op jit(solution)/shard_map/ppermute | solution.py:18
  71.2 33.1 %collective-permute-start.4 = (bf16[4,256]{1,0:T(4,128)(2,1)}, bf16[4,256]{1,0:T(4,128)(2,1)S(1)}, u32[]{:S(2)}, u32[]{:S(2)}) collective-permute-start(bf16[4,256]{1,0:T(4,128)(2,1)} %convert_element_type.264), channel_id=1, source_target_pairs={{496,0},{504,8},{0,16},{8,24},{16,32},{24,40},{32,48},{40,56},{48,... | collective-permute-start | bytes 6152 | tf_op jit(solution)/shard_map/ppermute | solution.py:18
  73.7 25.4 %collective-permute-start.3 = (bf16[4,256,128]{2,1,0:T(8,128)(2,1)}, bf16[4,256,128]{2,1,0:T(8,128)(2,1)S(1)}, u32[]{:S(2)}, u32[]{:S(2)}) collective-permute-start(bf16[4,256,128]{2,1,0:T(8,128)(2,1)} %bitcast.90), channel_id=1, source_target_pairs={{496,0},{504,8},{0,16},{8,24},{16,32},{24,40},{32,48},{40,56},{48,... | collective-permute-start | bytes 786440 | tf_op jit(solution)/shard_map/ppermute | solution.py:18
  79.0 48.9 %collective-permute-start.7 = (bf16[4,256]{1,0:T(4,128)(2,1)}, bf16[4,256]{1,0:T(4,128)(2,1)S(1)}, u32[]{:S(2)}, u32[]{:S(2)}) collective-permute-start(bf16[4,256]{1,0:T(4,128)(2,1)} %convert_element_type.264), channel_id=1, source_target_pairs={{488,0},{496,8},{504,16},{0,24},{8,32},{16,40},{24,48},{32,56},{40... | collective-permute-start | bytes 6152 | tf_op jit(solution)/shard_map/ppermute | solution.py:18
  85.0 35.4 %collective-permute-start.6 = (bf16[4,256,128]{2,1,0:T(8,128)(2,1)}, bf16[4,256,128]{2,1,0:T(8,128)(2,1)S(1)}, u32[]{:S(2)}, u32[]{:S(2)}) collective-permute-start(bf16[4,256,128]{2,1,0:T(8,128)(2,1)} %bitcast.90), channel_id=1, source_target_pairs={{488,0},{496,8},{504,16},{0,24},{8,32},{16,40},{24,48},{32,56},{40... | collective-permute-start | bytes 786440 | tf_op jit(solution)/shard_map/ppermute | solution.py:18
  87.6 58.5 %collective-permute-start.10 = (bf16[4,256]{1,0:T(4,128)(2,1)}, bf16[4,256]{1,0:T(4,128)(2,1)S(1)}, u32[]{:S(2)}, u32[]{:S(2)}) collective-permute-start(bf16[4,256]{1,0:T(4,128)(2,1)} %convert_element_type.264), channel_id=1, source_target_pairs={{480,0},{488,8},{496,16},{504,24},{0,32},{8,40},{16,48},{24,56},{3... | collective-permute-start | bytes 6152 | tf_op jit(solution)/shard_map/ppermute | solution.py:18
  99.2 44.3 %collective-permute-start.9 = (bf16[4,256,128]{2,1,0:T(8,128)(2,1)}, bf16[4,256,128]{2,1,0:T(8,128)(2,1)S(1)}, u32[]{:S(2)}, u32[]{:S(2)}) collective-permute-start(bf16[4,256,128]{2,1,0:T(8,128)(2,1)} %bitcast.90), channel_id=1, source_target_pairs={{480,0},{488,8},{496,16},{504,24},{0,32},{8,40},{16,48},{24,56},{3... | collective-permute-start | bytes 786440 | tf_op jit(solution)/shard_map/ppermute | solution.py:18
  104.3 58.5 %collective-permute-start.13 = (bf16[4,256]{1,0:T(4,128)(2,1)}, bf16[4,256]{1,0:T(4,128)(2,1)S(1)}, u32[]{:S(2)}, u32[]{:S(2)}) collective-permute-start(bf16[4,256]{1,0:T(4,128)(2,1)} %convert_element_type.264), channel_id=1, source_target_pairs={{32,0},{40,8},{48,16},{56,24},{64,32},{72,40},{80,48},{88,56},{96,... | collective-permute-start | bytes 6152 | tf_op jit(solution)/shard_map/ppermute | solution.py:18
  120.4 37.3 %collective-permute-start.12 = (bf16[4,256,128]{2,1,0:T(8,128)(2,1)}, bf16[4,256,128]{2,1,0:T(8,128)(2,1)S(1)}, u32[]{:S(2)}, u32[]{:S(2)}) collective-permute-start(bf16[4,256,128]{2,1,0:T(8,128)(2,1)} %bitcast.90), channel_id=1, source_target_pairs={{32,0},{40,8},{48,16},{56,24},{64,32},{72,40},{80,48},{88,56},{96,... | collective-permute-start | bytes 786440 | tf_op jit(solution)/shard_map/ppermute | solution.py:18
  127.9 49.9 %collective-permute-start.16 = (bf16[4,256]{1,0:T(4,128)(2,1)}, bf16[4,256]{1,0:T(4,128)(2,1)S(1)}, u32[]{:S(2)}, u32[]{:S(2)}) collective-permute-start(bf16[4,256]{1,0:T(4,128)(2,1)} %convert_element_type.264), channel_id=1, source_target_pairs={{24,0},{32,8},{40,16},{48,24},{56,32},{64,40},{72,48},{80,56},{88,... | collective-permute-start | bytes 6152 | tf_op jit(solution)/shard_map/ppermute | solution.py:18
  143.5 32.0 %collective-permute-start.15 = (bf16[4,256,128]{2,1,0:T(8,128)(2,1)}, bf16[4,256,128]{2,1,0:T(8,128)(2,1)S(1)}, u32[]{:S(2)}, u32[]{:S(2)}) collective-permute-start(bf16[4,256,128]{2,1,0:T(8,128)(2,1)} %bitcast.90), channel_id=1, source_target_pairs={{24,0},{32,8},{40,16},{48,24},{56,32},{64,40},{72,48},{80,56},{88,... | collective-permute-start | bytes 786440 | tf_op jit(solution)/shard_map/ppermute | solution.py:18
  146.1 41.7 %collective-permute-start.19 = (bf16[4,256]{1,0:T(4,128)(2,1)}, bf16[4,256]{1,0:T(4,128)(2,1)S(1)}, u32[]{:S(2)}, u32[]{:S(2)}) collective-permute-start(bf16[4,256]{1,0:T(4,128)(2,1)} %convert_element_type.264), channel_id=1, source_target_pairs={{16,0},{24,8},{32,16},{40,24},{48,32},{56,40},{64,48},{72,56},{80,... | collective-permute-start | bytes 6152 | tf_op jit(solution)/shard_map/ppermute | solution.py:18
  157.7 29.8 %collective-permute-start.18 = (bf16[4,256,128]{2,1,0:T(8,128)(2,1)}, bf16[4,256,128]{2,1,0:T(8,128)(2,1)S(1)}, u32[]{:S(2)}, u32[]{:S(2)}) collective-permute-start(bf16[4,256,128]{2,1,0:T(8,128)(2,1)} %bitcast.90), channel_id=1, source_target_pairs={{16,0},{24,8},{32,16},{40,24},{48,32},{56,40},{64,48},{72,56},{80,... | collective-permute-start | bytes 786440 | tf_op jit(solution)/shard_map/ppermute | solution.py:18
  162.8 35.9 %collective-permute-start.22 = (bf16[4,256]{1,0:T(4,128)(2,1)}, bf16[4,256]{1,0:T(4,128)(2,1)S(1)}, u32[]{:S(2)}, u32[]{:S(2)}) collective-permute-start(bf16[4,256]{1,0:T(4,128)(2,1)} %convert_element_type.264), channel_id=1, source_target_pairs={{8,0},{16,8},{24,16},{32,24},{40,32},{48,40},{56,48},{64,56},{72,6... | collective-permute-start | bytes 6152 | tf_op jit(solution)/shard_map/ppermute | solution.py:18
  175.5 21.9 %collective-permute-start.21 = (bf16[4,256,128]{2,1,0:T(8,128)(2,1)}, bf16[4,256,128]{2,1,0:T(8,128)(2,1)}, u32[]{:S(2)}, u32[]{:S(2)}) collective-permute-start(bf16[4,256,128]{2,1,0:T(8,128)(2,1)} %bitcast.90), channel_id=1, source_target_pairs={{8,0},{16,8},{24,16},{32,24},{40,32},{48,40},{56,48},{64,56},{72,6... | collective-permute-start | bytes 786440 | tf_op jit(solution)/shard_map/ppermute | solution.py:18
  (3 other events, 29.5 us)
where the time goes:
time: 335 us; the launch traced here: 331 us
  blocking collectives  108 us (32%)
  starting transfers between devices  101 us (30%)
  matrix products  60.8 us (18%)
  other arithmetic  45.7 us (14%)
  local copies, waits for them, and re-layouts  12.9 us (4%)
    psum x1, blocking collectives, local(): gram_matrix = lax.psum(gram_local, ('blk', 'grp'))  108 us
    ppermute x24, starting transfers between devices, passed_along(): return lax.ppermute(block, axis, route)  101 us
    dot_general x36, matrix products, tile_terms(): jnp.einsum('pe,cqe->cpq', row_points, col_points, preferred_element_type=...  51.8 us
    convert_element_type x36, other arithmetic, tile_terms(): row_scales.astype(jnp.float32)[None, :, None]  24.9 us
    dot_general x36, matrix products, tile_terms(): jnp.einsum('cpq,kcq->kp', weights, col_panel, preferred_element_type=jnp....  7.53 us
    gather x1, local copies, waits for them, and re-layouts, local(): partner = jnp.take_along_axis(own_points, partner_pos[:, :, None], axis=1)  6.76 us
  transfers between devices with their start and end apart: 24, of which 0 were waited for; matrix products, arithmetic and copies ran while one was open for 28% of the time, Pallas kernels for 0%

commit v1 on v0

v1 whole, which is shorter than its diff:
```python
import functools
import math

import jax
import jax.numpy as jnp
from jax import lax
from jax.experimental import pallas as pl
from jax.experimental.pallas import tpu as pltpu
from jax.sharding import PartitionSpec as P

E = 128
K = 64
BS = 256
SLOTS = 16
REACH = 4
NB = 4
ROWS = BS + 2 * K + 16
KP = K + 16
LOG2E = 1.4426950408889634
MESH = pl.DeviceIdType.MESH
F32 = jnp.float32
BF16 = jnp.bfloat16


def nt_dot(a, b, precision=None):
    return lax.dot_general(
        a, b, (((1,), (1,)), ((), ())), precision=precision, preferred_element_type=F32
    )


def split3(value):
    hi = value.astype(BF16).astype(F32)
    mid = (value - hi).astype(BF16).astype(F32)
    return hi, mid, value - hi - mid


def walk_kernel(
    sizes, pts, pan, sev, lists, counts, walked, gram_out,
    own, recv, xaug, apcol, acc, mask, gram, part, stage_a, stage_b, stage_c, full,
    ssem, rsem, asend, arecv,
):
    nb, ng, fb, hops = sizes
    fc = nb // fb
    steps = NB * hops
    me = lax.axis_index("blk")
    mg = lax.axis_index("grp")
    right = lax.rem(me + 1, nb)
    left = lax.rem(me + nb - 1, nb)
    lo = lax.rem(me, fb)
    high = me // fb

    def grp_peer(o):
        return lax.rem(mg + o, ng)

    def b_peer(o):
        return high * fb + lax.rem(lo + o, fb)

    def c_peer(o):
        return lax.rem(high + o, fc) * fb + lo

    partners = [(right, mg), (left, mg)]
    partners += [(me, grp_peer(o)) for o in range(1, ng)]
    partners += [(b_peer(o), mg) for o in range(1, fb)]
    partners += [(c_peer(o), mg) for o in range(1, fc)]
    barrier = pltpu.get_barrier_semaphore()
    for partner in partners:
        pl.semaphore_signal(barrier, inc=1, device_id=partner, device_id_type=MESH)

    lane = lax.broadcasted_iota(jnp.int32, (BS, E), 1)

    def prepare(b):
        cols = slice(b * BS, (b + 1) * BS)
        x = pts[0, cols, :]
        xf = x.astype(F32)
        place = jnp.broadcast_to(sev[0:1, cols].astype(F32), (E, BS)).T
        place = jnp.concatenate([place, place], axis=1).astype(jnp.int32)
        picked = (place == lax.broadcasted_iota(jnp.int32, (BS, BS), 1)).astype(F32).astype(BF16)
        partner = jnp.dot(picked, x, preferred_element_type=F32)
        diff = xf - partner
        scale = jnp.sqrt(jnp.sum(diff * diff, axis=1, keepdims=True) + 1e-06)
        scale = jnp.broadcast_to(scale, (BS, E)).astype(BF16).astype(F32)
        norm = jnp.broadcast_to(jnp.sum(xf * xf, axis=1, keepdims=True), (BS, E))
        hi, mid, low = split3(norm)
        zero = jnp.zeros_like(norm)
        stats = jnp.where(
            lane == 0, scale, jnp.where(lane == 1, hi, jnp.where(lane == 2, mid, jnp.where(lane == 3, low, zero)))
        ).T[0:8, :]
        own[b, 0:BS, :] = x
        own[b, BS : BS + K, :] = pan[0, :, b * BS : b * BS + E]
        own[b, BS + K : BS + 2 * K, :] = pan[0, :, b * BS + E : (b + 1) * BS]
        own[b, BS + 2 * K : ROWS, :] = jnp.concatenate([stats[:, :E], stats[:, E:]], axis=0).astype(BF16)
        extra = jnp.where(lane == 0, -hi, jnp.where(lane == 1, -mid, jnp.where(lane == 2, -low, zero)))
        xaug[b, :, 0:E] = (2.0 * xf).astype(BF16)
        xaug[b, :, E : 2 * E] = extra.astype(BF16)
        apcol[b, :, :] = LOG2E / scale

    def hop(d, slot, source):
        return pltpu.make_async_remote_copy(
            src_ref=source,
            dst_ref=recv.at[d, slot],
            send_sem=ssem.at[d, slot],
            recv_sem=rsem.at[d, slot],
            device_id=((right, left)[d], mg),
            device_id_type=MESH,
        )

    prepare(0)
    pl.semaphore_wait(barrier, len(partners))
    for b in range(NB):
        if b:
            prepare(b)
        for d in range(2):
            hop(d, b, own.at[b]).start()

    spot = lax.broadcasted_iota(jnp.int32, mask.shape[1:], 0)
    away = spot - NB
    second = away >= steps
    away = jnp.where(second, away - steps, away)
    dist = lax.shift_right_arithmetic(away, 2) + 1
    owner = me + jnp.where(second, dist, -dist)
    owner = jnp.where(owner < 0, owner + nb, jnp.where(owner >= nb, owner - nb, owner))
    ids = jnp.where(spot < NB, me, owner) * NB + (away & (NB - 1))
    for r in range(NB):
        row = me * NB + r
        found = jnp.zeros(ids.shape, jnp.int32)
        for s in range(SLOTS):
            entry = jnp.where(s < counts[0, row], lists[0, row, s], -1)
            found = jnp.where(ids == entry, 1, found)
        mask[r, :, :] = found

    acc[...] = jnp.zeros_like(acc)
    tail = (lane < 3).astype(F32).astype(BF16)
    ones = jnp.ones((KP - K, BS), BF16)

    def block(slab, spot_index):
        keys = jnp.concatenate([slab[0:BS, :], tail], axis=1)
        panel = jnp.concatenate([slab[BS : BS + K, :], slab[BS + K : BS + 2 * K, :]], axis=1)
        panel = jnp.concatenate([panel, ones], axis=0)
        stats = slab[BS + 2 * K : ROWS, :].astype(F32)
        stats = jnp.concatenate([stats[0:8, :], stats[8:16, :]], axis=1)
        aq = 1.0 / stats[0:1, :]
        nq = stats[1:2, :] + stats[2:3, :] + stats[3:4, :]
        for r in range(NB):
            cross = nt_dot(xaug[r], keys)
            ap = apcol[r]
            power = ((cross - nq) * aq) * jnp.concatenate([ap, ap], axis=1)
            weights = jnp.exp2(power).astype(BF16)
            carried = nt_dot(panel, weights)
            live = mask[r, pl.ds(spot_index, 1), :]
            live = jnp.concatenate([live, live], axis=1)
            acc[r, :, :] += jnp.where(live > 0, carried, 0.0)

    for b in range(NB):
        block(own.at[b], b)

    def arrive(t, carry):
        for d in range(2):
            hop(d, t, recv.at[d, t]).wait_recv()

            @pl.when(t < steps - NB)
            def _():
                hop(d, t + NB, recv.at[d, t]).start()

        for d in range(2):
            block(recv.at[d, t], NB + d * steps + t)
        return carry

    lax.fori_loop(0, steps, arrive, 0)

    for r in range(NB):
        cols = slice(r * BS, (r + 1) * BS)
        total = acc[r, :, :]
        walked[:, cols] = (pan[0, :, cols].astype(F32) + total[0:K, :]) / (1.0 + total[K : K + 1, :])
    flat = walked[...]
    gram[...] = jnp.concatenate(
        [nt_dot(flat, flat, lax.Precision.HIGHEST), jnp.zeros((K, E - K), F32)], axis=1
    )

    def sent(t, carry):
        for d in range(2):
            hop(d, t, recv.at[d, t]).wait_send()
        return carry

    share = K // ng

    def exchange(stage, size, source, target, peer):
        copies = []
        for o in range(1, size):
            copy = pltpu.make_async_remote_copy(
                src_ref=source(o),
                dst_ref=target,
                send_sem=asend.at[stage, o - 1],
                recv_sem=arecv.at[stage, o - 1],
                device_id=peer(o),
                device_id_type=MESH,
            )
            copy.start()
            copies.append(copy)
        return copies

    def summed(slots, size):
        total = slots[0]
        for i in range(1, size):
            total = total + slots[i]
        return total

    def mine(o):
        start = pl.multiple_of(grp_peer(o) * share, share)
        return gram.at[pl.ds(start, share), :]

    copies = exchange(0, ng, mine, stage_a.at[mg], lambda o: (me, grp_peer(o)))
    own_rows = pl.ds(pl.multiple_of(mg * share, share), share)
    stage_a[mg] = gram[own_rows, :]
    lax.fori_loop(0, steps, sent, 0)
    for copy in copies:
        copy.wait()
    part[0] = summed(stage_a, ng)
    copies = exchange(1, fb, lambda o: part.at[0], stage_b.at[lo], lambda o: (b_peer(o), mg))
    stage_b[lo] = part[0]
    for copy in copies:
        copy.wait()
    part[1] = summed(stage_b, fb)
    copies = exchange(2, fc, lambda o: part.at[1], stage_c.at[high], lambda o: (c_peer(o), mg))
    stage_c[high] = part[1]
    for copy in copies:
        copy.wait()
    part[2] = summed(stage_c, fc)
    copies = exchange(3, ng, lambda o: part.at[2], full.at[mg], lambda o: (me, grp_peer(o)))
    full[mg] = part[2]
    for copy in copies:
        copy.wait()
    for i in range(ng):
        gram_out[i * share : (i + 1) * share, :] = full[i]


def solve_kernel(root, gram, walked, ortho, r_factor):
    group = 8
    sub = lax.broadcasted_iota(jnp.int32, (group, E), 0)
    col = lax.broadcasted_iota(jnp.int32, (group, E), 1)
    tiles = []
    for i in range(K // group):
        unit = (col == sub + (K + i * group)).astype(F32)
        tiles.append(gram[i * group : (i + 1) * group, :] + unit)
    for j in range(K):
        at, inner = divmod(j, group)
        row = tiles[at][inner : inner + 1, :]
        row = row * (1.0 / row[:, j : j + 1])
        for i in range(at, K // group):
            factor = tiles[i][:, j : j + 1]
            if i == at:
                factor = jnp.where(sub[:, 0:1] > inner, factor, 0.0)
            tiles[i] = tiles[i] - factor * row
    inverse = []
    for i in range(K // group):
        diagonal = jnp.sum(jnp.where(col == sub + i * group, tiles[i], 0.0), axis=1, keepdims=True)
        scaled = tiles[i] * (1.0 / jnp.sqrt(diagonal))
        upper = jnp.where(col >= sub + i * group, scaled, 0.0)
        r_factor[i * group : (i + 1) * group, :] = upper[:, 0:K] * (1.0 / root)
        inverse.append(scaled[:, K : 2 * K] * root)
    inverse = jnp.concatenate(inverse, axis=0)
    ortho[0, :, :] = jnp.dot(
        inverse, walked[...], precision=lax.Precision.HIGHEST, preferred_element_type=F32
    )


def local(points, start_panel, seventh, neighbours, counts):
    nb = lax.axis_size("blk")
    ng = lax.axis_size("grp")
    fb = 2 ** ((nb.bit_length() - 1) // 2)
    hops = min(REACH, (nb - 1) // 2)
    pts = points.shape[1]
    share = K // ng
    steps = NB * hops
    vmem = pl.BlockSpec(memory_space=pltpu.VMEM)
    smem = pl.BlockSpec(memory_space=pltpu.SMEM)
    widest = max(ng, fb, nb // fb)
    walked, gram = pl.pallas_call(
        functools.partial(walk_kernel, (nb, ng, fb, hops)),
        out_shape=(
            jax.ShapeDtypeStruct((K, pts), F32),
            jax.ShapeDtypeStruct((K, E), F32),
        ),
        in_specs=[vmem, vmem, vmem, smem, smem],
        out_specs=(vmem, vmem),
        scratch_shapes=[
            pltpu.VMEM((NB, ROWS, E), BF16),
            pltpu.VMEM((2, steps, ROWS, E), BF16),
            pltpu.VMEM((NB, BS, 2 * E), BF16),
            pltpu.VMEM((NB, BS, E), F32),
            pltpu.VMEM((NB, KP, BS), F32),
            pltpu.VMEM((NB, 40, E), jnp.int32),
            pltpu.VMEM((K, E), F32),
            pltpu.VMEM((3, share, E), F32),
            pltpu.VMEM((ng, share, E), F32),
            pltpu.VMEM((fb, share, E), F32),
            pltpu.VMEM((nb // fb, share, E), F32),
            pltpu.VMEM((ng, share, E), F32),
            pltpu.SemaphoreType.DMA((2, steps)),
            pltpu.SemaphoreType.DMA((2, steps)),
            pltpu.SemaphoreType.DMA((4, widest)),
            pltpu.SemaphoreType.DMA((4, widest)),
        ],
        compiler_params=pltpu.CompilerParams(
            collective_id=0, has_side_effects=True, vmem_limit_bytes=32 * 1024 * 1024
        ),
        name="walk",
    )(points, start_panel, seventh, neighbours, counts)
    root = math.sqrt(pts * nb * ng)
    return pl.pallas_call(
        functools.partial(solve_kernel, root),
        out_shape=(
            jax.ShapeDtypeStruct((1, K, pts), F32),
            jax.ShapeDtypeStruct((K, K), F32),
        ),
        in_specs=[vmem, vmem],
        out_specs=(vmem, vmem),
        name="solve",
    )(gram, walked)


def solution(mesh):
    in_specs = (
        P("grp", "blk", None),
        P("grp", None, "blk"),
        P("grp", "blk"),
        P("grp", None, None),
        P("grp", None),
    )
    out_specs = (P("grp", None, "blk"), P())
    return jax.shard_map(local, mesh=mesh, in_specs=in_specs, out_specs=out_specs, check_vma=False)
```

time: 335 us -> 95 us (0.28); the launches traced: 331 us -> 94.8 us
  blocking collectives: 108 us -> 0 us
  starting transfers between devices: 101 us -> 0 us
  Pallas kernels: 0 us -> 90.9 us
  matrix products: 60.8 us -> 0 us
  other arithmetic: 45.7 us -> 0 us
  local copies, waits for them, and re-layouts: 12.9 us -> 3.17 us
    psum x1 -> x0, blocking collectives: 108 us -> none  [local(): gram_matrix = lax.psum(gram_local, ('blk', 'grp'))]
    ppermute x24 -> x0, starting transfers between devices: 101 us -> none  [passed_along(): return lax.ppermute(block, axis, route)]
    pallas_call x0 -> x2, Pallas kernels: none -> 90.9 us  [the longest x1 83.4 us: local(): pl.pallas_call(functools.partial(walk_kernel, (nb, ng, fb, hops)), out_sh...]
    dot_general x73 -> x0, matrix products: 59.7 us -> none  [the longest x36 51.8 us: tile_terms(): jnp.einsum('pe,cqe->cpq', row_points, col_points, preferred_element_type=...]
    convert_element_type x82 -> x0, other arithmetic: 27.8 us -> none  [the longest x36 24.9 us: tile_terms(): row_scales.astype(jnp.float32)[None, :, None]]
    another operation x4 -> x0, other arithmetic: 11.4 us -> none  [the longest x3 6.52 us: local(): lower_factor = jnp.linalg.cholesky(gram_matrix)]
    gather x1 -> x0, local copies, waits for them, and re-layouts: 6.76 us -> none  [local(): partner = jnp.take_along_axis(own_points, partner_pos[:, :, None], axis=1)]
    reduce_sum x9 -> x0, other arithmetic: 4.12 us -> none  [the longest x8 2.67 us: accumulate(): col_norms = jnp.sum(col_float * col_float, axis=-1)]
  transfers between devices with their start and end apart: 24 -> 0, of which waited for: 0 -> 0; matrix products, arithmetic and copies ran while one was open for 28% -> 0% of each run, Pallas kernels for 0% -> 0%
where the time goes in v1:
time: 95 us; the launch traced here: 94.8 us
  Pallas kernels  90.9 us (96%)
  local copies, waits for them, and re-layouts  3.17 us (3%)
    pallas_call x1, Pallas kernels, local(): pl.pallas_call(functools.partial(walk_kernel, (nb, ng, fb, hops)), out_sh...  83.4 us
    pallas_call x1, Pallas kernels, local(): pl.pallas_call(functools.partial(solve_kernel, root), out_shape=(jax.Shap...  7.5 us
    unnamed x13, local copies, waits for them, and re-layouts  3.17 us

profile of v1, /device:TPU:1, one launch (start us, length us, event | category | flops | bytes accessed | tf_op | source)
XLA Modules:
  0.0 94.8 jit_solution(9696580744481081754)
XLA Ops:
  0.6 0.0 copy-start.5
  0.6 0.0 copy-start.4
  0.7 0.0 copy-start.2
  0.7 0.9 copy.7.lists
  1.5 0.0 copy-done.5
  1.5 0.0 copy-done.4
  1.5 0.1 copy-done.2
  1.6 0.0 copy-start.1
  1.6 0.9 %copy-done.1 = bf16[1,1024,128]{2,1,0:T(8,128)(2,1)S(1)} copy-done((bf16[1,1024,128]{2,1,0:T(8,128)(2,1)S(1)}, bf16[1,1024,128]{2,1,0:T(8,128)(2,1)}, u32[]{:S(2)}) %copy-start.1) | copy-done | bytes 262168
  2.5 83.4 %walk.1 = (f32[64,1024]{1,0:T(8,128)S(1)}, f32[64,128]{1,0:T(8,128)S(1)}) custom-call(bf16[1,1024,128]{2,1,0:T(8,128)(2,1)S(1)} %copy-done.1, bf16[1,64,1024]{2,1,0:T(8,128)(2,1)S(1)} %copy-done.2, s32[1,1024]{1,0:T(1,128)S(1)} %copy-done.4, s32[1,256,16]{2,1,0:T(8,128)S(1)} %copy.7.lists, s32[1,256]{1,0:T(1,128)S(1)} %copy-done.5), custom_call_target="tpu_custom_call" | custom-call | tf_op jit(solution)/shard_map/walk/pallas_call | solution.py:277
  86.0 0.0 copy-start
  86.0 0.7 copy-done
  86.7 0.0 copy-start.3
  86.7 0.6 copy-done.3
  87.3 7.5 %solve.1 = (f32[1,64,1024]{2,1,0:T(8,128)}, f32[64,64]{1,0:T(8,128)}) custom-call(f32[64,128]{1,0:T(8,128)} %copy-done.3, f32[64,1024]{1,0:T(8,128)} %copy-done), custom_call_target="tpu_custom_call" | custom-call | tf_op jit(solution)/shard_map/solve/pallas_call | solution.py:309
Async XLA Ops:
  0.6 0.9 copy-start.5
  0.6 0.9 copy-start.4
  0.7 0.9 copy-start.2
  1.6 0.9 %copy-start.1 = (bf16[1,1024,128]{2,1,0:T(8,128)(2,1)S(1)}, bf16[1,1024,128]{2,1,0:T(8,128)(2,1)}, u32[]{:S(2)}) copy-start(bf16[1,1024,128]{2,1,0:T(8,128)(2,1)} %pts.1) | copy-start | bytes 786436
  86.0 0.7 copy-start
  86.7 0.6 copy-start.3

commit v2 on v1

v2 whole, which is shorter than its diff:
```python
import functools
import math

import jax
import jax.numpy as jnp
from jax import lax
from jax.experimental import pallas as pl
from jax.experimental.pallas import tpu as pltpu
from jax.sharding import PartitionSpec as P

E = 128
K = 64
BS = 256
SLOTS = 16
REACH = 4
NB = 4
ROWS = BS + 2 * K + 16
KP = K + 16
LOG2E = 1.4426950408889634
MESH = pl.DeviceIdType.MESH
F32 = jnp.float32
BF16 = jnp.bfloat16


def nt_dot(a, b, precision=None):
    return lax.dot_general(
        a, b, (((1,), (1,)), ((), ())), precision=precision, preferred_element_type=F32
    )


def split3(value):
    hi = value.astype(BF16).astype(F32)
    mid = (value - hi).astype(BF16).astype(F32)
    return hi, mid, value - hi - mid


def far_slots(listed):
    f0, f1, f2, f3 = listed
    n0, n1, n2, n3 = 1 - f0, 1 - f1, 1 - f2, 1 - f3
    first = (f0, n0 * f1, n0 * n1 * f2 * f3, jnp.zeros_like(f0))
    second = (jnp.zeros_like(f0), n3 * n2 * f1 * f0, n3 * f2, f3)
    return first, second


def walk_kernel(
    sizes, pts, pan, sev, lists, counts, walked, gram_out,
    own, recv, stage, xaug, apcol, acc, mask, pick, g3, s0, s1, s2, p3,
    isem, ssem, rsem, asend, arecv,
):
    nb, ng, nz, hops = sizes
    nx = nb // nz
    near = NB * (hops - 1)
    steps = near + 2
    me = lax.axis_index("blk")
    mg = lax.axis_index("grp")
    right = lax.rem(me + 1, nb)
    left = lax.rem(me + nb - 1, nb)
    zz = lax.rem(me, nz)
    xx = me // nz
    team = nx * ng
    rank = xx * ng + mg

    def team_peer(o):
        at = lax.rem(rank + o, team)
        return ((at // ng) * nz + zz, lax.rem(at, ng)), at

    def line_peer(o):
        return (xx * nz + lax.rem(zz + o, nz), mg)

    loads = []
    for b in range(NB):
        low = b * BS
        loads.append(
            [
                pltpu.make_async_copy(pts.at[0, low : low + BS, :], own.at[b, 0:BS, :], isem.at[b, 0]),
                pltpu.make_async_copy(
                    pan.at[0, :, low : low + E], own.at[b, BS : BS + K, :], isem.at[b, 1]
                ),
                pltpu.make_async_copy(
                    pan.at[0, :, low + E : low + BS], own.at[b, BS + K : BS + 2 * K, :], isem.at[b, 2]
                ),
            ]
        )
        for load in loads[b]:
            load.start()

    partners = [(right, mg), (left, mg)]
    partners += [team_peer(o)[0] for o in range(1, team)]
    partners += [line_peer(o) for o in range(1, nz)]
    barrier = pltpu.get_barrier_semaphore()
    for partner in partners:
        pl.semaphore_signal(barrier, inc=1, device_id=partner, device_id_type=MESH)

    lane = lax.broadcasted_iota(jnp.int32, (BS, E), 1)

    def prepare(b):
        for load in loads[b]:
            load.wait()
        x = own[b, 0:BS, :]
        xf = x.astype(F32)
        place = jnp.broadcast_to(sev[0:1, b * BS : (b + 1) * BS].astype(F32), (E, BS)).T
        place = jnp.concatenate([place, place], axis=1).astype(jnp.int32)
        picked = (place == lax.broadcasted_iota(jnp.int32, (BS, BS), 1)).astype(F32).astype(BF16)
        partner = jnp.dot(picked, x, preferred_element_type=F32)
        diff = xf - partner
        scale = jnp.sqrt(jnp.sum(diff * diff, axis=1, keepdims=True) + 1e-06)
        scale = jnp.broadcast_to(scale, (BS, E)).astype(BF16).astype(F32)
        norm = jnp.broadcast_to(jnp.sum(xf * xf, axis=1, keepdims=True), (BS, E))
        hi, mid, low = split3(norm)
        zero = jnp.zeros_like(norm)
        stats = jnp.where(
            lane == 0, scale, jnp.where(lane == 1, hi, jnp.where(lane == 2, mid, jnp.where(lane == 3, low, zero)))
        ).T[0:8, :]
        own[b, BS + 2 * K : ROWS, :] = jnp.concatenate([stats[:, :E], stats[:, E:]], axis=0).astype(BF16)
        extra = jnp.where(lane == 0, -hi, jnp.where(lane == 1, -mid, jnp.where(lane == 2, -low, zero)))
        xaug[b, :, 0:E] = (2.0 * xf).astype(BF16)
        xaug[b, :, E : 2 * E] = extra.astype(BF16)
        apcol[b, :, :] = LOG2E / scale

    def hop(d, slot, source):
        return pltpu.make_async_remote_copy(
            src_ref=source,
            dst_ref=recv.at[d, slot],
            send_sem=ssem.at[d, slot],
            recv_sem=rsem.at[d, slot],
            device_id=((right, left)[d], mg),
            device_id_type=MESH,
        )

    prepare(0)
    pl.semaphore_wait(barrier, len(partners))
    for b in range(NB):
        if b:
            prepare(b)
        for d in range(2):
            hop(d, b, own.at[b]).start()

    def wrapped(owner):
        return jnp.where(owner < 0, owner + nb, jnp.where(owner >= nb, owner - nb, owner))

    def found_in(ids, row, found):
        for s in range(SLOTS):
            entry = jnp.where(s < counts[0, row], lists[0, s, row], -1)
            found = jnp.where(ids == entry, 1, found)
        return found

    far = NB + 2 * near
    spot = lax.broadcasted_iota(jnp.int32, (mask.shape[1], E), 0)
    away = spot - NB
    second_half = away >= near
    dist = lax.shift_right_arithmetic(jnp.where(second_half, away - near, away), 2) + 1
    shift = jnp.where(second_half, dist, -dist)
    shift = jnp.where(spot >= far, jnp.where(spot >= far + NB, hops, -hops), shift)
    shift = jnp.where(spot < NB, 0, shift)
    ids = wrapped(me + shift) * NB + (spot & (NB - 1))
    founds = []
    for r in range(NB):
        found = found_in(ids, me * NB + r, jnp.zeros(ids.shape, jnp.int32))
        founds.append(found)
        mask[r, :, :] = found
    for d in range(2):
        rows = [[f[far + NB * d + c : far + NB * d + c + 1, :] for c in range(NB)] for f in founds]
        listed = [functools.reduce(jnp.maximum, [row[c] for row in rows]) for c in range(NB)]
        for at, chosen in enumerate(far_slots(listed)):
            for r in range(NB):
                live = sum(chosen[c] * rows[r][c] for c in range(NB))
                mask[r, far + 2 * d + at : far + 2 * d + at + 1, :] = live
    sub = lax.broadcasted_iota(jnp.int32, (8, E), 0)
    for d in range(2):
        toward = (right, left)[d]
        source = wrapped(me + (1 - hops, hops - 1)[d])
        blocks = source * NB + sub
        found = jnp.zeros((8, E), jnp.int32)
        for r in range(NB):
            found = found_in(blocks, toward * NB + r, found)
        for at, chosen in enumerate(far_slots([found[c : c + 1, :] for c in range(NB)])):
            for c in range(NB):
                pick[d, at, c, :, :] = chosen[c]

    acc[...] = jnp.zeros_like(acc)
    stage[...] = jnp.zeros_like(stage)
    tail = (lane < 3).astype(F32).astype(BF16)
    ones = jnp.ones((KP - K, BS), BF16)

    def block(slab, spot_index):
        keys = jnp.concatenate([slab[0:BS, :], tail], axis=1)
        panel = jnp.concatenate([slab[BS : BS + K, :], slab[BS + K : BS + 2 * K, :]], axis=1)
        panel = jnp.concatenate([panel, ones], axis=0)
        stats = slab[BS + 2 * K : ROWS, :].astype(F32)
        stats = jnp.concatenate([stats[0:8, :], stats[8:16, :]], axis=1)
        aq = 1.0 / stats[0:1, :]
        nq = stats[1:2, :] + stats[2:3, :] + stats[3:4, :]
        for r in range(NB):
            cross = nt_dot(xaug[r], keys)
            ap = apcol[r]
            power = ((cross - nq) * aq) * jnp.concatenate([ap, ap], axis=1)
            weights = jnp.exp2(power).astype(BF16)
            carried = nt_dot(panel, weights)
            live = mask[r, pl.ds(spot_index, 1), :]
            live = jnp.concatenate([live, live], axis=1)
            acc[r, :, :] += jnp.where(live > 0, carried, 0.0)

    def inside(b, carry):
        block(own.at[b], b)
        return carry

    lax.fori_loop(0, NB, inside, 0)

    def arrive(t, carry):
        last = t - (near - NB)
        for d in range(2):
            hop(d, t, recv.at[d, t]).wait_recv()

            @pl.when(t < near - NB)
            def _():
                hop(d, t + NB, recv.at[d, t]).start()

            for at, (low, high) in enumerate(((0, 2), (1, 3))):

                @pl.when(jnp.logical_and(last >= low, last <= high))
                def _():
                    wanted = pick[d, at, last]
                    kept = stage[d, at].astype(F32)
                    taken = jnp.where(wanted > 0, recv[d, t].astype(F32), kept)
                    stage[d, at] = taken.astype(BF16)

                @pl.when(last == high)
                def _():
                    hop(d, near + at, stage.at[d, at]).start()

        for d in range(2):
            block(recv.at[d, t], NB + d * near + t)
        return carry

    lax.fori_loop(0, near, arrive, 0)

    def arrive_far(t, carry):
        for d in range(2):
            hop(d, near + t, recv.at[d, near + t]).wait_recv()
        for d in range(2):
            block(recv.at[d, near + t], far + 2 * d + t)
        return carry

    lax.fori_loop(0, 2, arrive_far, 0)

    for r in range(NB):
        cols = slice(r * BS, (r + 1) * BS)
        total = acc[r, :, :]
        panel = jnp.concatenate([own[r, BS : BS + K, :], own[r, BS + K : BS + 2 * K, :]], axis=1)
        walked[:, cols] = (panel.astype(F32) + total[0:K, :]) / (1.0 + total[K : K + 1, :])
    flat = walked[...]
    gram = jnp.concatenate(
        [nt_dot(flat, flat, lax.Precision.HIGHEST), jnp.zeros((K, E - K), F32)], axis=1
    )

    def sent(t, carry):
        for d in range(2):
            hop(d, t, recv.at[d, t]).wait_send()
        return carry

    share = K // team

    def exchange(at, size, source, target, slot, peer):
        for o in range(1, size):
            pltpu.make_async_remote_copy(
                src_ref=source(o),
                dst_ref=target.at[slot],
                send_sem=asend.at[at],
                recv_sem=arecv.at[at],
                device_id=peer(o),
                device_id_type=MESH,
            ).start()

    def arrived(at, size, target):
        whole = target.at[pl.ds(0, size - 1)]
        return pltpu.make_async_remote_copy(
            src_ref=whole,
            dst_ref=whole,
            send_sem=asend.at[at],
            recv_sem=arecv.at[at],
            device_id=line_peer(1),
            device_id_type=MESH,
        )

    for i in range(team):
        g3[i] = gram[i * share : (i + 1) * share, :]
    exchange(0, team, lambda o: g3.at[team_peer(o)[1]], s0, rank, lambda o: team_peer(o)[0])
    s0[rank] = g3[rank]
    lax.fori_loop(0, steps, sent, 0)
    arrived(0, team, s0).wait_recv()
    p3[0] = jnp.sum(s0[...], axis=0)
    exchange(1, nz, lambda o: p3.at[0], s1, zz, line_peer)
    s1[zz] = p3[0]
    arrived(1, nz, s1).wait_recv()
    p3[1] = jnp.sum(s1[...], axis=0)
    exchange(2, team, lambda o: p3.at[1], s2, rank, lambda o: team_peer(o)[0])
    s2[rank] = p3[1]
    arrived(2, team, s2).wait_recv()
    for i in range(team):
        gram_out[i * share : (i + 1) * share, :] = s2[i]
    arrived(0, team, s0).wait_send()
    arrived(1, nz, s1).wait_send()
    arrived(2, team, s2).wait_send()


def solve_kernel(root, gram, walked, ortho, r_factor):
    group = 8
    count = K // group
    sub = lax.broadcasted_iota(jnp.int32, (group, E), 0)
    col = lax.broadcasted_iota(jnp.int32, (group, E), 1)
    tiles = []
    for i in range(count):
        unit = (col == sub + (K + i * group)).astype(F32)
        tiles.append(gram[i * group : (i + 1) * group, :] + unit)
    for at in range(count):
        base = at * group
        wide = {
            i: [jnp.broadcast_to(tiles[i][:, base + k : base + k + 1], (group, E)) for k in range(group)]
            for i in range(at, count)
        }
        for k in range(group):
            inverse = 1.0 / wide[at][k][k : k + 1, :]
            row = tiles[at][k : k + 1, :] * inverse
            later = {m: wide[at][m][k : k + 1, :] * inverse for m in range(k + 1, group)}
            for i in range(at, count):
                factor = wide[i][k]
                if i == at:
                    factor = jnp.where(sub > k, factor, 0.0)
                tiles[i] = tiles[i] - factor * row
                for m, value in later.items():
                    wide[i][m] = wide[i][m] - factor * value
    rows = []
    for i in range(count):
        diagonal = jnp.sum(jnp.where(col == sub + i * group, tiles[i], 0.0), axis=1, keepdims=True)
        scaled = tiles[i] * (1.0 / jnp.sqrt(diagonal))
        upper = jnp.where(col >= sub + i * group, scaled, 0.0)
        r_factor[i * group : (i + 1) * group, :] = upper[:, 0:K] * (1.0 / root)
        rows.append(scaled[:, K : 2 * K] * root)
    ortho[0, :, :] = jnp.dot(
        jnp.concatenate(rows, axis=0),
        walked[...],
        precision=lax.Precision.HIGHEST,
        preferred_element_type=F32,
    )


def local(points, start_panel, seventh, neighbours, counts):
    nb = lax.axis_size("blk")
    ng = lax.axis_size("grp")
    nz = max(nb // 4, 1)
    hops = min(REACH, (nb - 1) // 2)
    pts = points.shape[1]
    team = (nb // nz) * ng
    share = K // team
    steps = NB * (hops - 1) + 2
    vmem = pl.BlockSpec(memory_space=pltpu.VMEM)
    smem = pl.BlockSpec(memory_space=pltpu.SMEM)
    hbm = pl.BlockSpec(memory_space=pltpu.HBM)
    walked, gram = pl.pallas_call(
        functools.partial(walk_kernel, (nb, ng, nz, hops)),
        out_shape=(
            jax.ShapeDtypeStruct((K, pts), F32),
            jax.ShapeDtypeStruct((K, E), F32),
        ),
        in_specs=[hbm, hbm, vmem, smem, smem],
        out_specs=(vmem, vmem),
        scratch_shapes=[
            pltpu.VMEM((NB, ROWS, E), BF16),
            pltpu.VMEM((2, steps, ROWS, E), BF16),
            pltpu.VMEM((2, 2, ROWS, E), BF16),
            pltpu.VMEM((NB, BS, 2 * E), BF16),
            pltpu.VMEM((NB, BS, E), F32),
            pltpu.VMEM((NB, KP, BS), F32),
            pltpu.VMEM((NB, 40, E), jnp.int32),
            pltpu.VMEM((2, 2, NB, 1, E), jnp.int32),
            pltpu.VMEM((team, share, E), F32),
            pltpu.VMEM((team, share, E), F32),
            pltpu.VMEM((nz, share, E), F32),
            pltpu.VMEM((team, share, E), F32),
            pltpu.VMEM((2, share, E), F32),
            pltpu.SemaphoreType.DMA((NB, 3)),
            pltpu.SemaphoreType.DMA((2, steps)),
            pltpu.SemaphoreType.DMA((2, steps)),
            pltpu.SemaphoreType.DMA((3,)),
            pltpu.SemaphoreType.DMA((3,)),
        ],
        compiler_params=pltpu.CompilerParams(
            collective_id=0, has_side_effects=True, vmem_limit_bytes=32 * 1024 * 1024
        ),
        name="walk",
    )(
        pltpu.with_memory_space_constraint(points, pltpu.HBM),
        pltpu.with_memory_space_constraint(start_panel, pltpu.HBM),
        seventh,
        jnp.swapaxes(neighbours, 1, 2),
        counts,
    )
    root = math.sqrt(pts * nb * ng)
    return pl.pallas_call(
        functools.partial(solve_kernel, root),
        out_shape=(
            jax.ShapeDtypeStruct((1, K, pts), F32),
            jax.ShapeDtypeStruct((K, K), F32),
        ),
        in_specs=[vmem, vmem],
        out_specs=(vmem, vmem),
        compiler_params=pltpu.CompilerParams(vmem_limit_bytes=16 * 1024 * 1024),
        name="solve",
    )(gram, walked)


def solution(mesh):
    in_specs = (
        P("grp", "blk", None),
        P("grp", None, "blk"),
        P("grp", "blk"),
        P("grp", None, None),
        P("grp", None),
    )
    out_specs = (P("grp", None, "blk"), P())
    return jax.shard_map(local, mesh=mesh, in_specs=in_specs, out_specs=out_specs, check_vma=False)
```

time: 95 us -> 75.4 us (0.79)
  Pallas kernels: 90.9 us -> 72.4 us
  local copies, waits for them, and re-layouts: 3.17 us -> 2.08 us
    pallas_call x1, Pallas kernels: 83.4 us -> 69.7 us  [local(): pl.pallas_call(functools.partial(walk_kernel, (nb, ng, nz, hops)), out_sh...]
    pallas_call x1, Pallas kernels: 7.5 us -> 2.67 us  [local(): pl.pallas_call(functools.partial(solve_kernel, root), out_shape=(jax.Shap...]
    unnamed x13 -> x6, local copies, waits for them, and re-layouts: 3.17 us -> 2.08 us
where the time goes in v2:
time: 75.4 us; the launch traced here: 75.1 us
  Pallas kernels  72.4 us (96%)
  local copies, waits for them, and re-layouts  2.08 us (3%)
    pallas_call x1, Pallas kernels, local(): pl.pallas_call(functools.partial(walk_kernel, (nb, ng, nz, hops)), out_sh...  69.7 us
    pallas_call x1, Pallas kernels, local(): pl.pallas_call(functools.partial(solve_kernel, root), out_shape=(jax.Shap...  2.67 us
    unnamed x6, local copies, waits for them, and re-layouts  2.08 us

profile of v2, /device:TPU:1, one launch (start us, length us, event | category | flops | bytes accessed | tf_op | source)
XLA Modules:
  0.0 75.1 jit_solution(323394696887684505)
XLA Ops:
  0.6 0.0 copy-start.2
  0.6 0.7 copy-done.2
  1.3 0.0 copy-start
  1.3 0.7 copy-done
  2.0 0.0 copy-start.1
  2.0 0.7 copy-done.1
  2.7 69.7 %walk.1 = (f32[64,1024]{1,0:T(8,128)S(1)}, f32[64,128]{1,0:T(8,128)S(1)}) custom-call(bf16[1,1024,128]{2,1,0:T(8,128)(2,1)} %pts.1, bf16[1,64,1024]{2,1,0:T(8,128)(2,1)} %pan.1, s32[1,1024]{1,0:T(1,128)S(1)} %copy-done.1, s32[1,16,256]{2,1,0:T(8,128)S(1)} %bitcast.1, s32[1,256]{1,0:T(1,128)S(1)} %copy-done.2), custom_call_target="tpu_custom_call" | custom-call | tf_op jit(solution)/shard_map/walk/pallas_call | solution.py:359
  72.4 2.7 %solve.1 = (f32[1,64,1024]{2,1,0:T(8,128)}, f32[64,64]{1,0:T(8,128)}) custom-call(f32[64,128]{1,0:T(8,128)S(1)} %get-tuple-element.4.gram, f32[64,1024]{1,0:T(8,128)S(1)} %get-tuple-element.5.walked), custom_call_target="tpu_custom_call" | custom-call | tf_op jit(solution)/shard_map/solve/pallas_call | solution.py:399
Async XLA Ops:
  0.6 0.7 copy-start.2
  1.3 0.7 copy-start
  2.0 0.7 copy-start.1

commit v3 on v2

--- a/solution.py
+++ b/solution.py
@@ -43,9 +43,9 @@
 
 
 def walk_kernel(
-    sizes, pts, pan, sev, lists, counts, walked, gram_out,
-    own, recv, stage, xaug, apcol, acc, mask, pick, g3, s0, s1, s2, p3,
-    isem, ssem, rsem, asend, arecv,
+    sizes, pts, pan, sev_in, lists_in, counts_in, walked, gram_out,
+    sev, lists, counts, own, recv, stage, xaug, apcol, acc, mask, pick, g3, s0, s1, s2, p3,
+    isem, ssem, rsem, asend, arecv, heard,
 ):
     nb, ng, nz, hops = sizes
     nx = nb // nz
@@ -60,13 +60,31 @@
     team = nx * ng
     rank = xx * ng + mg
 
+    yy = mg // 2
+    core = lax.rem(mg, 2)
+    ny = ng // 2
+
     def team_peer(o):
-        at = lax.rem(rank + o, team)
-        return ((at // ng) * nz + zz, lax.rem(at, ng)), at
+        gx = lax.rem(xx + o[0], nx)
+        gg = lax.rem(yy + o[1], ny) * 2 + lax.rem(core + o[2], 2)
+        return (gx * nz + zz, gg), gx * ng + gg
 
     def line_peer(o):
         return (xx * nz + lax.rem(zz + o, nz), mg)
 
+    def away_by(o, size):
+        return min(o, size - o)
+
+    team_offsets = [(a, b, c) for a in range(nx) for b in range(ny) for c in range(2)][1:]
+    team_offsets.sort(key=lambda o: (-away_by(o[0], nx) - away_by(o[1], ny), o))
+    line_offsets = sorted(range(1, nz), key=lambda o: (-away_by(o, nz), o))
+
+    small = [
+        pltpu.make_async_copy(sev_in, sev, isem.at[0, 3]),
+        pltpu.make_async_copy(lists_in.at[0], lists, isem.at[1, 3]),
+        pltpu.make_async_copy(counts_in, counts, isem.at[2, 3]),
+    ]
+    small[0].start()
     loads = []
     for b in range(NB):
         low = b * BS
@@ -84,9 +102,26 @@
         for load in loads[b]:
             load.start()
 
-    partners = [(right, mg), (left, mg)]
-    partners += [team_peer(o)[0] for o in range(1, team)]
-    partners += [line_peer(o) for o in range(1, nz)]
+    small[1].start()
+    small[2].start()
+
+    next_to = [line_peer(1), line_peer(nz - 1)]
+    next_to += [team_peer(o)[0] for o in ((1, 0, 0), (nx - 1, 0, 0), (0, 1, 0), (0, ny - 1, 0), (0, 0, 1))]
+    partners = [(right, mg), (left, mg)] + next_to
+    rounds = [
+        next_to,
+        [line_peer(2), line_peer(nz - 2)]
+        + [team_peer(o)[0] for o in ((2, 0, 0), (0, 2, 0), (1, 0, 0), (nx - 1, 0, 0))],
+        [line_peer(4), line_peer(nz - 4), team_peer((0, 0, 1))[0]],
+    ]
+
+    def vouch(at):
+        for partner in rounds[at]:
+            pl.semaphore_signal(heard.at[at], inc=1, device_id=partner, device_id_type=MESH)
+
+    def hear(at):
+        pl.semaphore_wait(heard.at[at], len(rounds[at]))
+
     barrier = pltpu.get_barrier_semaphore()
     for partner in partners:
         pl.semaphore_signal(barrier, inc=1, device_id=partner, device_id_type=MESH)
@@ -127,6 +162,7 @@
             device_id_type=MESH,
         )
 
+    small[0].wait()
     prepare(0)
     pl.semaphore_wait(barrier, len(partners))
     for b in range(NB):
@@ -134,13 +170,16 @@
             prepare(b)
         for d in range(2):
             hop(d, b, own.at[b]).start()
+    vouch(0)
+    small[1].wait()
+    small[2].wait()
 
     def wrapped(owner):
         return jnp.where(owner < 0, owner + nb, jnp.where(owner >= nb, owner - nb, owner))
 
     def found_in(ids, row, found):
         for s in range(SLOTS):
-            entry = jnp.where(s < counts[0, row], lists[0, s, row], -1)
+            entry = jnp.where(s < counts[0, row], lists[s, row], -1)
             found = jnp.where(ids == entry, 1, found)
         return found
 
@@ -208,6 +247,13 @@
 
     def arrive(t, carry):
         last = t - (near - NB)
+        for at in range(2):
+
+            @pl.when(t == NB * (at + 1))
+            def _():
+                hear(at)
+                vouch(at + 1)
+
         for d in range(2):
             hop(d, t, recv.at[d, t]).wait_recv()
 
@@ -233,6 +279,7 @@
         return carry
 
     lax.fori_loop(0, near, arrive, 0)
+    hear(2)
 
     def arrive_far(t, carry):
         for d in range(2):
@@ -260,8 +307,8 @@
 
     share = K // team
 
-    def exchange(at, size, source, target, slot, peer):
-        for o in range(1, size):
+    def exchange(at, offsets, source, target, slot, peer):
+        for o in offsets:
             pltpu.make_async_remote_copy(
                 src_ref=source(o),
                 dst_ref=target.at[slot],
@@ -284,16 +331,16 @@
 
     for i in range(team):
         g3[i] = gram[i * share : (i + 1) * share, :]
-    exchange(0, team, lambda o: g3.at[team_peer(o)[1]], s0, rank, lambda o: team_peer(o)[0])
+    exchange(0, team_offsets, lambda o: g3.at[team_peer(o)[1]], s0, rank, lambda o: team_peer(o)[0])
     s0[rank] = g3[rank]
     lax.fori_loop(0, steps, sent, 0)
     arrived(0, team, s0).wait_recv()
     p3[0] = jnp.sum(s0[...], axis=0)
-    exchange(1, nz, lambda o: p3.at[0], s1, zz, line_peer)
+    exchange(1, line_offsets, lambda o: p3.at[0], s1, zz, line_peer)
     s1[zz] = p3[0]
     arrived(1, nz, s1).wait_recv()
     p3[1] = jnp.sum(s1[...], axis=0)
-    exchange(2, team, lambda o: p3.at[1], s2, rank, lambda o: team_peer(o)[0])
+    exchange(2, team_offsets, lambda o: p3.at[1], s2, rank, lambda o: team_peer(o)[0])
     s2[rank] = p3[1]
     arrived(2, team, s2).wait_recv()
     for i in range(team):
@@ -354,7 +401,6 @@
     share = K // team
     steps = NB * (hops - 1) + 2
     vmem = pl.BlockSpec(memory_space=pltpu.VMEM)
-    smem = pl.BlockSpec(memory_space=pltpu.SMEM)
     hbm = pl.BlockSpec(memory_space=pltpu.HBM)
     walked, gram = pl.pallas_call(
         functools.partial(walk_kernel, (nb, ng, nz, hops)),
@@ -362,9 +408,12 @@
             jax.ShapeDtypeStruct((K, pts), F32),
             jax.ShapeDtypeStruct((K, E), F32),
         ),
-        in_specs=[hbm, hbm, vmem, smem, smem],
+        in_specs=[hbm] * 5,
         out_specs=(vmem, vmem),
         scratch_shapes=[
+            pltpu.VMEM((1, pts), jnp.int32),
+            pltpu.SMEM(neighbours.shape[:0:-1], jnp.int32),
+            pltpu.SMEM(counts.shape, jnp.int32),
             pltpu.VMEM((NB, ROWS, E), BF16),
             pltpu.VMEM((2, steps, ROWS, E), BF16),
             pltpu.VMEM((2, 2, ROWS, E), BF16),
@@ -378,22 +427,22 @@
             pltpu.VMEM((nz, share, E), F32),
             pltpu.VMEM((team, share, E), F32),
             pltpu.VMEM((2, share, E), F32),
-            pltpu.SemaphoreType.DMA((NB, 3)),
+            pltpu.SemaphoreType.DMA((NB, 4)),
             pltpu.SemaphoreType.DMA((2, steps)),
             pltpu.SemaphoreType.DMA((2, steps)),
             pltpu.SemaphoreType.DMA((3,)),
             pltpu.SemaphoreType.DMA((3,)),
+            pltpu.SemaphoreType.REGULAR((3,)),
         ],
         compiler_params=pltpu.CompilerParams(
             collective_id=0, has_side_effects=True, vmem_limit_bytes=32 * 1024 * 1024
         ),
         name="walk",
     )(
-        pltpu.with_memory_space_constraint(points, pltpu.HBM),
-        pltpu.with_memory_space_constraint(start_panel, pltpu.HBM),
-        seventh,
-        jnp.swapaxes(neighbours, 1, 2),
-        counts,
+        *(
+            pltpu.with_memory_space_constraint(each, pltpu.HBM)
+            for each in (points, start_panel, seventh, jnp.swapaxes(neighbours, 1, 2), counts)
+        )
     )
     root = math.sqrt(pts * nb * ng)
     return pl.pallas_call(

time: 75.4 us -> 68.2 us (0.905)
  Pallas kernels: 72.4 us -> 67.4 us
  local copies, waits for them, and re-layouts: 2.08 us -> 0 us
    pallas_call x1, Pallas kernels: 69.7 us -> 64.8 us  [local(): pl.pallas_call(functools.partial(walk_kernel, (nb, ng, nz, hops)), out_sh...]
    unnamed x6 -> x0, local copies, waits for them, and re-layouts: 2.08 us -> none
where the time goes in v3:
time: 68.2 us; the launch traced here: 68.1 us
  Pallas kernels  67.4 us (99%)
    pallas_call x1, Pallas kernels, local(): pl.pallas_call(functools.partial(walk_kernel, (nb, ng, nz, hops)), out_sh...  64.8 us
    pallas_call x1, Pallas kernels, local(): pl.pallas_call(functools.partial(solve_kernel, root), out_shape=(jax.Shap...  2.67 us

profile of v3, /device:TPU:1, one launch (start us, length us, event | category | flops | bytes accessed | tf_op | source)
XLA Modules:
  0.0 68.1 jit_solution(11863488936075406591)
XLA Ops:
  0.6 64.8 %walk.1 = (f32[64,1024]{1,0:T(8,128)S(1)}, f32[64,128]{1,0:T(8,128)S(1)}) custom-call(bf16[1,1024,128]{2,1,0:T(8,128)(2,1)} %pts.1, bf16[1,64,1024]{2,1,0:T(8,128)(2,1)} %pan.1, s32[1,1024]{1,0:T(1,128)} %sev_in.1, s32[1,16,256]{2,1,0:T(8,128)} %bitcast.1, s32[1,256]{1,0:T(1,128)} %counts_in.1), custom_call_target="tpu_custom_call" | custom-call | tf_op jit(solution)/shard_map/walk/pallas_call | solution.py:405
  65.4 2.7 %solve.1 = (f32[1,64,1024]{2,1,0:T(8,128)}, f32[64,64]{1,0:T(8,128)}) custom-call(f32[64,128]{1,0:T(8,128)S(1)} %get-tuple-element.4.gram, f32[64,1024]{1,0:T(8,128)S(1)} %get-tuple-element.5.walked), custom_call_target="tpu_custom_call" | custom-call | tf_op jit(solution)/shard_map/solve/pallas_call | solution.py:448

commit v4 on v3

--- a/solution.py
+++ b/solution.py
@@ -12,7 +12,6 @@
 K = 64
 BS = 256
 SLOTS = 16
-REACH = 4
 NB = 4
 ROWS = BS + 2 * K + 16
 KP = K + 16
@@ -44,12 +43,12 @@
 
 def walk_kernel(
     sizes, pts, pan, sev_in, lists_in, counts_in, walked, gram_out,
-    sev, lists, counts, own, recv, stage, xaug, apcol, acc, mask, pick, g3, s0, s1, s2, p3,
-    isem, ssem, rsem, asend, arecv, heard,
+    sev, lists, counts, own, recv, stage, xaug, apcol, acc, mask, pick, rout, rin, g3, s0, s1, s2, p3,
+    isem, ssem, rsem, osem, nsem, asend, arecv, heard,
 ):
-    nb, ng, nz, hops = sizes
+    nb, ng, nz = sizes
     nx = nb // nz
-    near = NB * (hops - 1)
+    near = 2 * NB
     steps = near + 2
     me = lax.axis_index("blk")
     mg = lax.axis_index("grp")
@@ -143,14 +142,25 @@
         norm = jnp.broadcast_to(jnp.sum(xf * xf, axis=1, keepdims=True), (BS, E))
         hi, mid, low = split3(norm)
         zero = jnp.zeros_like(norm)
-        stats = jnp.where(
-            lane == 0, scale, jnp.where(lane == 1, hi, jnp.where(lane == 2, mid, jnp.where(lane == 3, low, zero)))
-        ).T[0:8, :]
+        columns = jnp.where(
+            lane == 0, hi, jnp.where(lane == 1, mid, jnp.where(lane == 2, low, jnp.where(lane == 3, scale, zero)))
+        )
+        stats = columns.T[0:8, :]
         own[b, BS + 2 * K : ROWS, :] = jnp.concatenate([stats[:, :E], stats[:, E:]], axis=0).astype(BF16)
-        extra = jnp.where(lane == 0, -hi, jnp.where(lane == 1, -mid, jnp.where(lane == 2, -low, zero)))
-        xaug[b, :, 0:E] = (2.0 * xf).astype(BF16)
-        xaug[b, :, E : 2 * E] = extra.astype(BF16)
-        apcol[b, :, :] = LOG2E / scale
+        keep_rows(0, b, xf, columns, scale)
+
+    def keep_rows(who, b, xf, columns, scale):
+        xaug[who, b, :, 0:E] = (2.0 * xf).astype(BF16)
+        xaug[who, b, :, E : 2 * E] = jnp.where(lane < 3, -columns, 0.0).astype(BF16)
+        apcol[who, b, :, :] = LOG2E / scale
+
+    def row_stats(slab):
+        stats = slab[BS + 2 * K : ROWS, :].astype(F32)
+        return jnp.concatenate([stats[0:8, :], stats[8:16, :]], axis=1)
+
+    def adopt(who, b, slab):
+        columns = jnp.concatenate([row_stats(slab)] * (E // 8), axis=0).T
+        keep_rows(who, b, slab[0:BS, :].astype(F32), columns, jnp.broadcast_to(columns[:, 3:4], (BS, E)))
 
     def hop(d, slot, source):
         return pltpu.make_async_remote_copy(
@@ -183,35 +193,29 @@
             found = jnp.where(ids == entry, 1, found)
         return found
 
-    far = NB + 2 * near
-    spot = lax.broadcasted_iota(jnp.int32, (mask.shape[1], E), 0)
+    spot = lax.broadcasted_iota(jnp.int32, (mask.shape[2], E), 0)
     away = spot - NB
-    second_half = away >= near
-    dist = lax.shift_right_arithmetic(jnp.where(second_half, away - near, away), 2) + 1
-    shift = jnp.where(second_half, dist, -dist)
-    shift = jnp.where(spot >= far, jnp.where(spot >= far + NB, hops, -hops), shift)
-    shift = jnp.where(spot < NB, 0, shift)
+    dist = lax.shift_right_arithmetic(jnp.where(away >= near, away - near, away), 2) + 1
+    shift = jnp.where(spot < NB, 0, jnp.where(away >= near, dist, -dist))
     ids = wrapped(me + shift) * NB + (spot & (NB - 1))
-    founds = []
     for r in range(NB):
-        found = found_in(ids, me * NB + r, jnp.zeros(ids.shape, jnp.int32))
-        founds.append(found)
-        mask[r, :, :] = found
-    for d in range(2):
-        rows = [[f[far + NB * d + c : far + NB * d + c + 1, :] for c in range(NB)] for f in founds]
-        listed = [functools.reduce(jnp.maximum, [row[c] for row in rows]) for c in range(NB)]
-        for at, chosen in enumerate(far_slots(listed)):
-            for r in range(NB):
-                live = sum(chosen[c] * rows[r][c] for c in range(NB))
-                mask[r, far + 2 * d + at : far + 2 * d + at + 1, :] = live
+        mask[0, r, :, :] = found_in(ids, me * NB + r, jnp.zeros(ids.shape, jnp.int32))
     sub = lax.broadcasted_iota(jnp.int32, (8, E), 0)
     for d in range(2):
         toward = (right, left)[d]
-        source = wrapped(me + (1 - hops, hops - 1)[d])
-        blocks = source * NB + sub
+        side = 2 * d - 1
+        ids = wrapped(me + jnp.where(sub < NB, 2 * side, 3 * side)) * NB + (sub & (NB - 1))
+        founds = [found_in(ids, toward * NB + r, jnp.zeros((8, E), jnp.int32)) for r in range(NB)]
+        rows = [[f[NB + c : NB + c + 1, :] for c in range(NB)] for f in founds]
+        listed = [functools.reduce(jnp.maximum, [row[c] for row in rows]) for c in range(NB)]
+        for r in range(NB):
+            mask[1 + d, r, 0:8, :] = founds[r]
+            for at, chosen in enumerate(far_slots(listed)):
+                mask[1 + d, r, NB + at : NB + at + 1, :] = sum(chosen[c] * rows[r][c] for c in range(NB))
+        blocks = wrapped(me + 2 * side) * NB + sub
         found = jnp.zeros((8, E), jnp.int32)
         for r in range(NB):
-            found = found_in(blocks, toward * NB + r, found)
+            found = found_in(blocks, wrapped(me - 2 * side) * NB + r, found)
         for at, chosen in enumerate(far_slots([found[c : c + 1, :] for c in range(NB)])):
             for c in range(NB):
                 pick[d, at, c, :, :] = chosen[c]
@@ -221,78 +225,119 @@
     tail = (lane < 3).astype(F32).astype(BF16)
     ones = jnp.ones((KP - K, BS), BF16)
 
-    def block(slab, spot_index):
+    def block(slab, who, spot_index):
         keys = jnp.concatenate([slab[0:BS, :], tail], axis=1)
         panel = jnp.concatenate([slab[BS : BS + K, :], slab[BS + K : BS + 2 * K, :]], axis=1)
         panel = jnp.concatenate([panel, ones], axis=0)
-        stats = slab[BS + 2 * K : ROWS, :].astype(F32)
-        stats = jnp.concatenate([stats[0:8, :], stats[8:16, :]], axis=1)
-        aq = 1.0 / stats[0:1, :]
-        nq = stats[1:2, :] + stats[2:3, :] + stats[3:4, :]
+        stats = row_stats(slab)
+        aq = 1.0 / stats[3:4, :]
+        nq = stats[0:1, :] + stats[1:2, :] + stats[2:3, :]
         for r in range(NB):
-            cross = nt_dot(xaug[r], keys)
-            ap = apcol[r]
+            cross = nt_dot(xaug[who, r], keys)
+            ap = apcol[who, r]
             power = ((cross - nq) * aq) * jnp.concatenate([ap, ap], axis=1)
             weights = jnp.exp2(power).astype(BF16)
             carried = nt_dot(panel, weights)
-            live = mask[r, pl.ds(spot_index, 1), :]
+            live = mask[who, r, pl.ds(spot_index, 1), :]
             live = jnp.concatenate([live, live], axis=1)
-            acc[r, :, :] += jnp.where(live > 0, carried, 0.0)
+            acc[who, r, :, :] += jnp.where(live > 0, carried, 0.0)
 
     def inside(b, carry):
-        block(own.at[b], b)
+        block(own.at[b], 0, b)
         return carry
 
     lax.fori_loop(0, NB, inside, 0)
 
-    def arrive(t, carry):
-        last = t - (near - NB)
-        for at in range(2):
-
-            @pl.when(t == NB * (at + 1))
-            def _():
-                hear(at)
-                vouch(at + 1)
-
+    def first_hop(t, carry):
         for d in range(2):
             hop(d, t, recv.at[d, t]).wait_recv()
-
-            @pl.when(t < near - NB)
-            def _():
-                hop(d, t + NB, recv.at[d, t]).start()
-
+            hop(d, t + NB, recv.at[d, t]).start()
+
+        @pl.when(t == NB - 1)
+        def _():
+            hear(0)
+            vouch(1)
+
+        for d in range(2):
+            block(recv.at[d, t], 0, NB + d * near + t)
+            adopt(2 - d, t, recv.at[d, t])
+        return carry
+
+    lax.fori_loop(0, NB, first_hop, 0)
+
+    def second_hop(c, carry):
+        t = c + NB
+        for d in range(2):
+            hop(d, t, recv.at[d, t]).wait_recv()
             for at, (low, high) in enumerate(((0, 2), (1, 3))):
 
-                @pl.when(jnp.logical_and(last >= low, last <= high))
+                @pl.when(jnp.logical_and(c >= low, c <= high))
                 def _():
-                    wanted = pick[d, at, last]
+                    wanted = pick[d, at, c]
                     kept = stage[d, at].astype(F32)
                     taken = jnp.where(wanted > 0, recv[d, t].astype(F32), kept)
                     stage[d, at] = taken.astype(BF16)
 
-                @pl.when(last == high)
+                @pl.when(c == high)
                 def _():
                     hop(d, near + at, stage.at[d, at]).start()
 
-        for d in range(2):
-            block(recv.at[d, t], NB + d * near + t)
+        @pl.when(c == 2)
+        def _():
+            hear(1)
+            vouch(2)
+
+        for d in range(2):
+            block(recv.at[d, t], 1 + d, c)
         return carry
 
-    lax.fori_loop(0, near, arrive, 0)
+    lax.fori_loop(0, NB, second_hop, 0)
+
+    def third_hop(at, carry):
+        for d in range(2):
+            hop(d, near + at, recv.at[d, near + at]).wait_recv()
+        for d in range(2):
+            block(recv.at[d, near + at], 1 + d, NB + at)
+        return carry
+
+    lax.fori_loop(0, 2, third_hop, 0)
+
+    def result(d, r):
+        return pltpu.make_async_remote_copy(
+            src_ref=rout.at[d, r],
+            dst_ref=rin.at[d, r],
+            send_sem=osem.at[d, r],
+            recv_sem=nsem.at[d, r],
+            device_id=((right, left)[d], mg),
+            device_id_type=MESH,
+        )
+
+    rest = lax.broadcasted_iota(jnp.int32, (KP - K, BS), 0)
+    for r in range(NB):
+        for d in range(2):
+            degree = acc[1 + d, r, K:KP, :]
+            high = degree.astype(BF16).astype(F32)
+            degree = jnp.where(rest == 0, high, jnp.where(rest == 1, degree - high, 0.0))
+            rout[d, r, 0:K, :] = acc[1 + d, r, 0:K, :].astype(BF16)
+            rout[d, r, K:KP, :] = degree.astype(BF16)
+            result(d, r).start()
+
+    def own_rows_later(t, carry):
+        for d in range(2):
+            block(recv.at[d, t], 0, NB + d * near + t)
+        return carry
+
+    lax.fori_loop(NB, near, own_rows_later, 0)
     hear(2)
-
-    def arrive_far(t, carry):
-        for d in range(2):
-            hop(d, near + t, recv.at[d, near + t]).wait_recv()
-        for d in range(2):
-            block(recv.at[d, near + t], far + 2 * d + t)
-        return carry
-
-    lax.fori_loop(0, 2, arrive_far, 0)
 
     for r in range(NB):
         cols = slice(r * BS, (r + 1) * BS)
-        total = acc[r, :, :]
+        total = acc[0, r, 0 : K + 8, :]
+        for d in range(2):
+            result(d, r).wait_recv()
+            more = rin[d, r, :, :].astype(F32)
+            extra = more[K : K + 1, :] + more[K + 1 : K + 2, :]
+            total = total + jnp.concatenate([more[0:K, :], jnp.broadcast_to(extra, (8, BS))], axis=0)
         panel = jnp.concatenate([own[r, BS : BS + K, :], own[r, BS + K : BS + 2 * K, :]], axis=1)
         walked[:, cols] = (panel.astype(F32) + total[0:K, :]) / (1.0 + total[K : K + 1, :])
     flat = walked[...]
@@ -304,6 +349,10 @@
         for d in range(2):
             hop(d, t, recv.at[d, t]).wait_send()
         return carry
+
+    for d in range(2):
+        for r in range(NB):
+            result(d, r).wait_send()
 
     share = K // team
 
@@ -395,15 +444,14 @@
     nb = lax.axis_size("blk")
     ng = lax.axis_size("grp")
     nz = max(nb // 4, 1)
-    hops = min(REACH, (nb - 1) // 2)
     pts = points.shape[1]
     team = (nb // nz) * ng
     share = K // team
-    steps = NB * (hops - 1) + 2
+    steps = 2 * NB + 2
     vmem = pl.BlockSpec(memory_space=pltpu.VMEM)
     hbm = pl.BlockSpec(memory_space=pltpu.HBM)
     walked, gram = pl.pallas_call(
-        functools.partial(walk_kernel, (nb, ng, nz, hops)),
+        functools.partial(walk_kernel, (nb, ng, nz)),
         out_shape=(
             jax.ShapeDtypeStruct((K, pts), F32),
             jax.ShapeDtypeStruct((K, E), F32),
@@ -417,11 +465,13 @@
             pltpu.VMEM((NB, ROWS, E), BF16),
             pltpu.VMEM((2, steps, ROWS, E), BF16),
             pltpu.VMEM((2, 2, ROWS, E), BF16),
-            pltpu.VMEM((NB, BS, 2 * E), BF16),
-            pltpu.VMEM((NB, BS, E), F32),
-            pltpu.VMEM((NB, KP, BS), F32),
-            pltpu.VMEM((NB, 40, E), jnp.int32),
+            pltpu.VMEM((3, NB, BS, 2 * E), BF16),
+            pltpu.VMEM((3, NB, BS, E), F32),
+            pltpu.VMEM((3, NB, KP, BS), F32),
+            pltpu.VMEM((3, NB, 24, E), jnp.int32),
             pltpu.VMEM((2, 2, NB, 1, E), jnp.int32),
+            pltpu.VMEM((2, NB, KP, BS), BF16),
+            pltpu.VMEM((2, NB, KP, BS), BF16),
             pltpu.VMEM((team, share, E), F32),
             pltpu.VMEM((team, share, E), F32),
             pltpu.VMEM((nz, share, E), F32),
@@ -430,6 +480,8 @@
             pltpu.SemaphoreType.DMA((NB, 4)),
             pltpu.SemaphoreType.DMA((2, steps)),
             pltpu.SemaphoreType.DMA((2, steps)),
+            pltpu.SemaphoreType.DMA((2, NB)),
+            pltpu.SemaphoreType.DMA((2, NB)),
             pltpu.SemaphoreType.DMA((3,)),
             pltpu.SemaphoreType.DMA((3,)),
             pltpu.SemaphoreType.REGULAR((3,)),

time: 68.2 us -> 65.2 us (0.956)
  Pallas kernels: 67.4 us -> 64.4 us
    pallas_call x1, Pallas kernels: 64.8 us -> 61.7 us  [local(): pl.pallas_call(functools.partial(walk_kernel, (nb, ng, nz)), out_shape=(j...]
where the time goes in v4:
time: 65.2 us; the launch traced here: 65.1 us
  Pallas kernels  64.4 us (99%)
    pallas_call x1, Pallas kernels, local(): pl.pallas_call(functools.partial(walk_kernel, (nb, ng, nz)), out_shape=(j...  61.7 us
    pallas_call x1, Pallas kernels, local(): pl.pallas_call(functools.partial(solve_kernel, root), out_shape=(jax.Shap...  2.67 us

profile of v4, /device:TPU:1, one launch (start us, length us, event | category | flops | bytes accessed | tf_op | source)
XLA Modules:
  0.0 65.1 jit_solution(11030827780096570373)
XLA Ops:
  0.6 61.7 %walk.1 = (f32[64,1024]{1,0:T(8,128)S(1)}, f32[64,128]{1,0:T(8,128)S(1)}) custom-call(bf16[1,1024,128]{2,1,0:T(8,128)(2,1)} %pts.1, bf16[1,64,1024]{2,1,0:T(8,128)(2,1)} %pan.1, s32[1,1024]{1,0:T(1,128)} %sev_in.1, s32[1,16,256]{2,1,0:T(8,128)} %bitcast.1, s32[1,256]{1,0:T(1,128)} %counts_in.1), custom_call_target="tpu_custom_call" | custom-call | tf_op jit(solution)/shard_map/walk/pallas_call | solution.py:453
  62.4 2.7 %solve.1 = (f32[1,64,1024]{2,1,0:T(8,128)}, f32[64,64]{1,0:T(8,128)}) custom-call(f32[64,128]{1,0:T(8,128)S(1)} %get-tuple-element.4.gram, f32[64,1024]{1,0:T(8,128)S(1)} %get-tuple-element.5.walked), custom_call_target="tpu_custom_call" | custom-call | tf_op jit(solution)/shard_map/solve/pallas_call | solution.py:500

commit v5 on v4

--- a/solution.py
+++ b/solution.py
@@ -13,8 +13,8 @@
 BS = 256
 SLOTS = 16
 NB = 4
-ROWS = BS + 2 * K + 16
-KP = K + 16
+ROWS = BS + 2 * K + 8
+KP = K + 8
 LOG2E = 1.4426950408889634
 MESH = pl.DeviceIdType.MESH
 F32 = jnp.float32
@@ -145,7 +145,7 @@
         columns = jnp.where(
             lane == 0, hi, jnp.where(lane == 1, mid, jnp.where(lane == 2, low, jnp.where(lane == 3, scale, zero)))
         )
-        stats = columns.T[0:8, :]
+        stats = columns.T[0:4, :]
         own[b, BS + 2 * K : ROWS, :] = jnp.concatenate([stats[:, :E], stats[:, E:]], axis=0).astype(BF16)
         keep_rows(0, b, xf, columns, scale)
 
@@ -156,10 +156,10 @@
 
     def row_stats(slab):
         stats = slab[BS + 2 * K : ROWS, :].astype(F32)
-        return jnp.concatenate([stats[0:8, :], stats[8:16, :]], axis=1)
+        return jnp.concatenate([stats[0:4, :], stats[4:8, :]], axis=1)
 
     def adopt(who, b, slab):
-        columns = jnp.concatenate([row_stats(slab)] * (E // 8), axis=0).T
+        columns = jnp.concatenate([row_stats(slab)] * (E // 4), axis=0).T
         keep_rows(who, b, slab[0:BS, :].astype(F32), columns, jnp.broadcast_to(columns[:, 3:4], (BS, E)))
 
     def hop(d, slot, source):
@@ -341,9 +341,9 @@
         panel = jnp.concatenate([own[r, BS : BS + K, :], own[r, BS + K : BS + 2 * K, :]], axis=1)
         walked[:, cols] = (panel.astype(F32) + total[0:K, :]) / (1.0 + total[K : K + 1, :])
     flat = walked[...]
-    gram = jnp.concatenate(
-        [nt_dot(flat, flat, lax.Precision.HIGHEST), jnp.zeros((K, E - K), F32)], axis=1
-    )
+    gram = nt_dot(flat, jnp.concatenate([flat, flat], axis=0), lax.Precision.HIGHEST)
+    half = lax.broadcasted_iota(jnp.int32, (K // 2, E), 1) < K
+    packed = jnp.where(half, gram[0 : K // 2, :], gram[K // 2 : K, :])
 
     def sent(t, carry):
         for d in range(2):
@@ -354,7 +354,8 @@
         for r in range(NB):
             result(d, r).wait_send()
 
-    share = K // team
+    share = K // 2 // ng
+    grp_offsets = [o for o in team_offsets if o[0] == 0]
 
     def exchange(at, offsets, source, target, slot, peer):
         for o in offsets:
@@ -378,12 +379,14 @@
             device_id_type=MESH,
         )
 
-    for i in range(team):
-        g3[i] = gram[i * share : (i + 1) * share, :]
-    exchange(0, team_offsets, lambda o: g3.at[team_peer(o)[1]], s0, rank, lambda o: team_peer(o)[0])
-    s0[rank] = g3[rank]
+    for i in range(ng):
+        g3[i] = packed[i * share : (i + 1) * share, :]
+    exchange(
+        0, grp_offsets, lambda o: g3.at[team_peer(o)[0][1]], s0, mg, lambda o: team_peer(o)[0]
+    )
+    s0[mg] = g3[mg]
     lax.fori_loop(0, steps, sent, 0)
-    arrived(0, team, s0).wait_recv()
+    arrived(0, ng, s0).wait_recv()
     p3[0] = jnp.sum(s0[...], axis=0)
     exchange(1, line_offsets, lambda o: p3.at[0], s1, zz, line_peer)
     s1[zz] = p3[0]
@@ -392,9 +395,16 @@
     exchange(2, team_offsets, lambda o: p3.at[1], s2, rank, lambda o: team_peer(o)[0])
     s2[rank] = p3[1]
     arrived(2, team, s2).wait_recv()
-    for i in range(team):
-        gram_out[i * share : (i + 1) * share, :] = s2[i]
-    arrived(0, team, s0).wait_send()
+    whole = []
+    for i in range(ng):
+        part = s2[i]
+        for x in range(1, nx):
+            part = part + s2[x * ng + i]
+        whole.append(part)
+    whole = jnp.concatenate(whole, axis=0)
+    gram_out[0 : K // 2, :] = jnp.where(half, whole, 0.0)
+    gram_out[K // 2 : K, :] = jnp.where(half, pltpu.roll(whole, K, 1), 0.0)
+    arrived(0, ng, s0).wait_send()
     arrived(1, nz, s1).wait_send()
     arrived(2, team, s2).wait_send()
 
@@ -446,7 +456,7 @@
     nz = max(nb // 4, 1)
     pts = points.shape[1]
     team = (nb // nz) * ng
-    share = K // team
+    share = K // 2 // ng
     steps = 2 * NB + 2
     vmem = pl.BlockSpec(memory_space=pltpu.VMEM)
     hbm = pl.BlockSpec(memory_space=pltpu.HBM)
@@ -472,8 +482,8 @@
             pltpu.VMEM((2, 2, NB, 1, E), jnp.int32),
             pltpu.VMEM((2, NB, KP, BS), BF16),
             pltpu.VMEM((2, NB, KP, BS), BF16),
-            pltpu.VMEM((team, share, E), F32),
-            pltpu.VMEM((team, share, E), F32),
+            pltpu.VMEM((ng, share, E), F32),
+            pltpu.VMEM((ng, share, E), F32),
             pltpu.VMEM((nz, share, E), F32),
             pltpu.VMEM((team, share, E), F32),
             pltpu.VMEM((2, share, E), F32),

time: 65.2 us -> 64.3 us (0.986)
  Pallas kernels: 64.4 us -> 63.5 us
    pallas_call x1, Pallas kernels: 61.7 us -> 60.9 us  [local(): pl.pallas_call(functools.partial(walk_kernel, (nb, ng, nz)), out_shape=(j...]
where the time goes in v5:
time: 64.3 us; the launch traced here: 64.2 us
  Pallas kernels  63.5 us (99%)
    pallas_call x1, Pallas kernels, local(): pl.pallas_call(functools.partial(walk_kernel, (nb, ng, nz)), out_shape=(j...  60.9 us
    pallas_call x1, Pallas kernels, local(): pl.pallas_call(functools.partial(solve_kernel, root), out_shape=(jax.Shap...  2.67 us

profile of v5, /device:TPU:1, one launch (start us, length us, event | category | flops | bytes accessed | tf_op | source)
XLA Modules:
  0.0 64.2 jit_solution(15627898452816182678)
XLA Ops:
  0.6 60.9 %walk.1 = (f32[64,1024]{1,0:T(8,128)S(1)}, f32[64,128]{1,0:T(8,128)S(1)}) custom-call(bf16[1,1024,128]{2,1,0:T(8,128)(2,1)} %pts.1, bf16[1,64,1024]{2,1,0:T(8,128)(2,1)} %pan.1, s32[1,1024]{1,0:T(1,128)} %sev_in.1, s32[1,16,256]{2,1,0:T(8,128)} %bitcast.1, s32[1,256]{1,0:T(1,128)} %counts_in.1), custom_call_target="tpu_custom_call" | custom-call | tf_op jit(solution)/shard_map/walk/pallas_call | solution.py:463
  61.5 2.7 %solve.1 = (f32[1,64,1024]{2,1,0:T(8,128)}, f32[64,64]{1,0:T(8,128)}) custom-call(f32[64,128]{1,0:T(8,128)S(1)} %get-tuple-element.4.gram, f32[64,1024]{1,0:T(8,128)S(1)} %get-tuple-element.5.walked), custom_call_target="tpu_custom_call" | custom-call | tf_op jit(solution)/shard_map/solve/pallas_call | solution.py:510

commit v6 on v5

--- a/solution.py
+++ b/solution.py
@@ -98,11 +98,8 @@
                 ),
             ]
         )
-        for load in loads[b]:
-            load.start()
-
-    small[1].start()
-    small[2].start()
+    for load in loads[0]:
+        load.start()
 
     next_to = [line_peer(1), line_peer(nz - 1)]
     next_to += [team_peer(o)[0] for o in ((1, 0, 0), (nx - 1, 0, 0), (0, 1, 0), (0, ny - 1, 0), (0, 0, 1))]
@@ -124,6 +121,11 @@
     barrier = pltpu.get_barrier_semaphore()
     for partner in partners:
         pl.semaphore_signal(barrier, inc=1, device_id=partner, device_id_type=MESH)
+    for b in range(1, NB):
+        for load in loads[b]:
+            load.start()
+    small[1].start()
+    small[2].start()
 
     lane = lax.broadcasted_iota(jnp.int32, (BS, E), 1)
 

time: 64.3 us -> 64.3 us (level)
  no operation moved by 1% of the time
where the time goes in v6:
time: 64.3 us; the launch traced here: 64.1 us
  Pallas kernels  63.5 us (99%)
    pallas_call x1, Pallas kernels, local(): pl.pallas_call(functools.partial(walk_kernel, (nb, ng, nz)), out_shape=(j...  60.8 us
    pallas_call x1, Pallas kernels, local(): pl.pallas_call(functools.partial(solve_kernel, root), out_shape=(jax.Shap...  2.67 us

profile of v6, /device:TPU:1, one launch (start us, length us, event | category | flops | bytes accessed | tf_op | source)
XLA Modules:
  0.0 64.1 jit_solution(14477072499588368045)
XLA Ops:
  0.6 60.8 %walk.1 = (f32[64,1024]{1,0:T(8,128)S(1)}, f32[64,128]{1,0:T(8,128)S(1)}) custom-call(bf16[1,1024,128]{2,1,0:T(8,128)(2,1)} %pts.1, bf16[1,64,1024]{2,1,0:T(8,128)(2,1)} %pan.1, s32[1,1024]{1,0:T(1,128)} %sev_in.1, s32[1,16,256]{2,1,0:T(8,128)} %bitcast.1, s32[1,256]{1,0:T(1,128)} %counts_in.1), custom_call_target="tpu_custom_call" | custom-call | tf_op jit(solution)/shard_map/walk/pallas_call | solution.py:465
  61.5 2.7 %solve.1 = (f32[1,64,1024]{2,1,0:T(8,128)}, f32[64,64]{1,0:T(8,128)}) custom-call(f32[64,128]{1,0:T(8,128)S(1)} %get-tuple-element.4.gram, f32[64,1024]{1,0:T(8,128)S(1)} %get-tuple-element.5.walked), custom_call_target="tpu_custom_call" | custom-call | tf_op jit(solution)/shard_map/solve/pallas_call | solution.py:512
